TPU v7x, 128 devices: a whole 4x4x4 slice. The times are simulated.
128 devices in a mesh: shot: 4 (over x_hi, core), gx: 4 (over z), gy: 8 (over x_lo, y).
Axes of the slice: x: 4 (x_hi: 2, x_lo: 2; x = x_hi * 2 + x_lo), y: 4, z: 4, core: 2. Of those that a mesh axis runs over, the one named last changes fastest.
Arguments:
- velocity: bfloat16 [512, 256, 256], P(('shot', 'gx'), 'gy'), may hold values from 0.14941406 to 0.34960938
- epsilon: bfloat16 [512, 256, 256], P(('shot', 'gx'), 'gy'), may hold values from 0.049804688 to 0.29882812
- delta: bfloat16 [512, 256, 256], P(('shot', 'gx'), 'gy'), may hold values from 0.019897461 to 0.14941406
- anchors: int32 [4], replicated, may hold values from 0 to 384
- sources: int32 [4, 3], P('shot'), may hold values from 0 to 255, as said below
- wavelet: float32 [4, 4], P('shot'), may hold values from -8 to 8
- p_now: float32 [4, 128, 256, 256], P('shot', 'gx', 'gy'), may hold values from -6 to 6
- p_prev: float32 [4, 128, 256, 256], P('shot', 'gx', 'gy'), may hold values from -6 to 6
- q_now: float32 [4, 128, 256, 256], P('shot', 'gx', 'gy'), may hold values from -6 to 6
- q_prev: float32 [4, 128, 256, 256], P('shot', 'gx', 'gy'), may hold values from -6 to 6
Outputs:
- p_out: float32 [4, 128, 256, 256], P('shot', 'gx', 'gy')
- q_out: float32 [4, 128, 256, 256], P('shot', 'gx', 'gy')
Inputs may be any that keep to these rules, and one draw needn't show every extreme that they name: `sources`: each source lies inside its aperture: x below 128, y below 256, z below 256; some source lies on the aperture's far end along its longest dimension, and some source has x equal to 0.
All inputs are finite; a program needn't handle non-finite values.
Results may differ from a plain program's by a relative error of at most 0.0003.
Values may be sent and summed in bfloat16 or wider, within the bound.
A program may use at most 128 MiB of HBM per device.

v0:
```python
import jax
import jax.numpy as jnp
from jax import lax
from jax.sharding import PartitionSpec as P

STEPS = 4


STENCIL_WEIGHTS = (-205.0 / 72.0, 8.0 / 5.0, -1.0 / 5.0, 8.0 / 315.0, -1.0 / 560.0)


def with_halo(block, sides, width):
    for axis, dim in sides:
        count = lax.axis_size(axis)
        forward = [(i, i + 1) for i in range(count - 1)]
        backward = [(target, source) for source, target in forward]
        low = lax.ppermute(
            lax.slice_in_dim(block, block.shape[dim] - width, None, axis=dim), axis, forward
        )
        high = lax.ppermute(lax.slice_in_dim(block, 0, width, axis=dim), axis, backward)
        block = jnp.concatenate([low, block, high], axis=dim)
    return block


def shifted_up(values, reach):
    filler = jnp.zeros(values.shape[:-1] + (reach,), values.dtype)
    return jnp.concatenate([values[..., reach:], filler], -1)


def shifted_down(values, reach):
    filler = jnp.zeros(values.shape[:-1] + (reach,), values.dtype)
    return jnp.concatenate([filler, values[..., :-reach]], -1)


def vertical_second(values):
    total = STENCIL_WEIGHTS[0] * values
    for reach in range(1, 5):
        total = total + STENCIL_WEIGHTS[reach] * (
            shifted_up(values, reach) + shifted_down(values, reach)
        )
    return total


def horizontal_second(padded, x_count, y_count):
    x_total = STENCIL_WEIGHTS[0] * padded[4 : 4 + x_count, 4 : 4 + y_count]
    for reach in range(1, 5):
        x_total = x_total + STENCIL_WEIGHTS[reach] * (
            padded[4 + reach : 4 + reach + x_count, 4 : 4 + y_count]
            + padded[4 - reach : 4 - reach + x_count, 4 : 4 + y_count]
        )
    y_total = STENCIL_WEIGHTS[0] * padded[4 : 4 + x_count, 4 : 4 + y_count]
    for reach in range(1, 5):
        y_total = y_total + STENCIL_WEIGHTS[reach] * (
            padded[4 : 4 + x_count, 4 + reach : 4 + reach + y_count]
            + padded[4 : 4 + x_count, 4 - reach : 4 - reach + y_count]
        )
    return x_total + y_total


def update(padded_p, p_field, p_before, q_field, q_before, courant_sq, horiz_gain, cross_gain):
    laplace_h = horizontal_second(padded_p, p_field.shape[0], p_field.shape[1])
    depth_term = vertical_second(q_field)
    p_next = (
        2.0 * p_field - p_before + courant_sq * (horiz_gain * laplace_h + cross_gain * depth_term)
    )
    q_next = 2.0 * q_field - q_before + courant_sq * (cross_gain * laplace_h + depth_term)
    return (p_next, q_next)


def window_rows(pieces, offset, row_count):
    total_rows = pieces.shape[0]
    padded = jnp.pad(pieces, ((row_count, row_count), (0, 0), (0, 0)))
    begin_at = jnp.clip(offset + row_count, 0, total_rows + row_count)
    return lax.dynamic_slice_in_dim(padded, begin_at, row_count, 0)


def source_mask(sources, x_count, y_count, z_count, x_first, y_first):
    x_match = (jnp.arange(x_count, dtype=jnp.int32) + x_first == sources[0, 0]).astype(jnp.float32)
    y_match = (jnp.arange(y_count, dtype=jnp.int32) + y_first == sources[0, 1]).astype(jnp.float32)
    z_match = (jnp.arange(z_count, dtype=jnp.int32) == sources[0, 2]).astype(jnp.float32)
    return x_match[:, None, None] * y_match[None, :, None] * z_match[None, None, :]


def on_device(velocity, epsilon, delta, anchors, sources, wavelet, p_now, p_prev, q_now, q_prev):
    x_cells = p_now.shape[1]
    y_cells = p_now.shape[2]
    z_cells = p_now.shape[3]
    shot_index = lax.axis_index("shot")
    x_index = lax.axis_index("gx")
    y_index = lax.axis_index("gy")
    base_row = anchors[shot_index] + x_index * x_cells
    pieces = (
        lax.all_gather(velocity, ("shot", "gx"), axis=0, tiled=True),
        lax.all_gather(epsilon, ("shot", "gx"), axis=0, tiled=True),
        lax.all_gather(delta, ("shot", "gx"), axis=0, tiled=True),
    )
    velocity_block, epsilon_block, delta_block = tuple(
        (window_rows(piece_one, base_row, x_cells) for piece_one in pieces)
    )
    courant_sq = velocity_block.astype(jnp.float32) * velocity_block.astype(jnp.float32)
    horiz_gain = 1.0 + 2.0 * epsilon_block.astype(jnp.float32)
    cross_gain = jnp.sqrt(1.0 + 2.0 * delta_block.astype(jnp.float32))
    x_first = x_index * x_cells
    y_first = y_index * y_cells
    inner_source = source_mask(sources, x_cells, y_cells, z_cells, x_first, y_first)
    p_field = p_now[0]
    p_before = p_prev[0]
    q_field = q_now[0]
    q_before = q_prev[0]
    for step_index in range(STEPS):
        padded = with_halo(p_field, (("gx", 0), ("gy", 1)), 4)
        p_next, q_next = update(
            padded, p_field, p_before, q_field, q_before, courant_sq, horiz_gain, cross_gain
        )
        p_next = p_next + wavelet[0, step_index] * inner_source
        p_before, p_field, q_before, q_field = (p_field, p_next, q_field, q_next)
    return (p_field[None], q_field[None])


def solution(mesh):
    return jax.shard_map(
        on_device,
        mesh=mesh,
        in_specs=(
            P(("shot", "gx"), "gy", None),
            P(("shot", "gx"), "gy", None),
            P(("shot", "gx"), "gy", None),
            P(),
            P("shot", None),
            P("shot", None),
            P("shot", "gx", "gy", None),
            P("shot", "gx", "gy", None),
            P("shot", "gx", "gy", None),
            P("shot", "gx", "gy", None),
        ),
        out_specs=(P("shot", "gx", "gy", None), P("shot", "gx", "gy", None)),
        check_vma=False,
    )
```

profile of v0, /device:TPU:2, one launch (start us, length us, event | category | flops | bytes accessed | tf_op | source)
XLA Modules:
  0.0 381.0 jit_solution(8481441208767258015)
XLA Ops:
  9.4 3.8 %collective-permute-start.1 = (f32[4,32,256]{2,1,0:T(8,128)S(1)}, f32[4,32,256]{2,1,0:T(8,128)S(1)}, u32[]{:S(2)}, u32[]{:S(2)}) collective-permute-start(f32[4,32,256]{2,1,0:T(8,128)S(1)} %get-tuple-element.68), channel_id=1, source_target_pairs={{0,8},{8,16},{16,24},{1,9},{9,17},{17,25},{2,10},{10,18},{18,26},{... | collective-permute-start | bytes 393224 | tf_op jit(solution)/shard_map/ppermute | solution.py:17
  23.4 4.9 %collective-permute-start.2 = (f32[40,4,256]{2,1,0:T(4,128)S(1)}, f32[40,4,256]{2,1,0:T(4,128)S(1)}, u32[]{:S(2)}, u32[]{:S(2)}) collective-permute-start(f32[40,4,256]{2,1,0:T(4,128)S(1)} %get-tuple-element.28), channel_id=1, source_target_pairs={{1,0},{2,1},{3,2},{4,3},{5,4},{6,5},{7,6},{9,8},{10,9},{11,10},{12... | collective-permute-start | bytes 491528 | tf_op jit(solution)/shard_map/ppermute | solution.py:20
  32.8 4.9 %collective-permute-done.3 = f32[40,4,256]{2,1,0:T(4,128)S(1)} collective-permute-done((f32[40,4,256]{2,1,0:T(4,128)S(1)}, f32[40,4,256]{2,1,0:T(4,128)S(1)}, u32[]{:S(2)}, u32[]{:S(2)}) %collective-permute-start.3) | collective-permute-done | bytes 163872 | tf_op jit(solution)/shard_map/ppermute | solution.py:17
  39.7 45.4 %all-gather.4.cloned.1.call-done = bf16[512,32,256]{2,1,0:T(8,128)(2,1)} async-done(((bf16[32,32,256]{2,1,0:T(8,128)(2,1)}), bf16[512,32,256]{2,1,0:T(8,128)(2,1)}) %all-gather.4.cloned.1.call-update) | async-done | bytes 8388624 | tf_op jit(solution)/shard_map/all_gather | solution.py:93
  85.1 73.3 %all-gather.6.cloned.1.call-done = bf16[512,32,256]{2,1,0:T(8,128)(2,1)} async-done(((bf16[32,32,256]{2,1,0:T(8,128)(2,1)}), bf16[512,32,256]{2,1,0:T(8,128)(2,1)}) %all-gather.6.cloned.1.call-update) | async-done | bytes 8388624 | tf_op jit(solution)/shard_map/all_gather | solution.py:94
  158.5 73.3 %all-gather.8.cloned.1.call-done = bf16[512,32,256]{2,1,0:T(8,128)(2,1)} async-done(((bf16[32,32,256]{2,1,0:T(8,128)(2,1)}), bf16[512,32,256]{2,1,0:T(8,128)(2,1)}) %all-gather.8.cloned.1.call-update) | async-done | bytes 8388624 | tf_op jit(solution)/shard_map/all_gather | solution.py:95
  231.8 12.9 %fusion.68 = (f32[32,32,256]{2,1,0:T(8,128)S(1)}, f32[32,32,256]{2,1,0:T(8,128)S(1)}, f32[32,32,256]{2,1,0:T(8,128)}) fusion(f32[1,32,32,256]{3,2,1,0:T(8,128)} %param.17, f32[256]{0:T(256)S(1)} %compare_convert_fusion, f32[32,32]{1,0:T(8,128)S(1)} %broadcast_multiply_fusion, f32[]{:T(128)} %bitcast.6, f32[1,32,32,256]{3,2,1,0:T(8,128)S(1)} %copy-done.1, ...), kind=kLoop, calls=%fused_computation.131 | loop fusion | flops 17039360 | bytes 49468424 | tf_op jit(solution)/shard_map/add | solution.py:115
  244.7 2.8 fusion.113
  256.0 4.1 %collective-permute-done.4 = f32[4,32,256]{2,1,0:T(8,128)S(1)} collective-permute-done((f32[4,32,256]{2,1,0:T(8,128)S(1)}, f32[4,32,256]{2,1,0:T(8,128)S(1)}, u32[]{:S(2)}, u32[]{:S(2)}) %collective-permute-start.4) | collective-permute-done | bytes 131104 | tf_op jit(solution)/shard_map/ppermute | solution.py:20
  260.2 5.5 %collective-permute-start.6 = (f32[40,4,256]{2,1,0:T(4,128)S(1)}, f32[40,4,256]{2,1,0:T(4,128)S(1)}, u32[]{:S(2)}, u32[]{:S(2)}) collective-permute-start(f32[40,4,256]{2,1,0:T(4,128)S(1)} %get-tuple-element.24), channel_id=1, source_target_pairs={{1,0},{2,1},{3,2},{4,3},{5,4},{6,5},{7,6},{9,8},{10,9},{11,10},{12... | collective-permute-start | bytes 491528 | tf_op jit(solution)/shard_map/ppermute | solution.py:20
  269.5 5.5 %collective-permute-done.7 = f32[40,4,256]{2,1,0:T(4,128)S(1)} collective-permute-done((f32[40,4,256]{2,1,0:T(4,128)S(1)}, f32[40,4,256]{2,1,0:T(4,128)S(1)}, u32[]{:S(2)}, u32[]{:S(2)}) %collective-permute-start.7) | collective-permute-done | bytes 163872 | tf_op jit(solution)/shard_map/ppermute | solution.py:17
  277.0 12.1 %fusion.69 = (f32[32,32,256]{2,1,0:T(8,128)S(1)}, f32[32,32,256]{2,1,0:T(8,128)}, f32[32,32,256]{2,1,0:T(8,128)}) fusion(f32[32,32,256]{2,1,0:T(8,128)S(1)} %get-tuple-element.11, f32[]{:T(128)} %bitcast.11, f32[256]{0:T(256)S(1)} %compare_convert_fusion, f32[32,32]{1,0:T(8,128)S(1)} %broadcast_multiply_fusion, f32[1,32,32,256]{3,2,1,0:T(8,128)S(1)} %copy-done.1, ...), kind=kLoop, calls=%fused_computation.132 | loop fusion | flops 17039360 | bytes 48419848 | tf_op jit(solution)/shard_map/add | solution.py:115
  289.2 2.4 multiply_add_fusion.3
  295.0 3.3 collective-permute-start.9
  301.3 3.9 %collective-permute-done.8 = f32[4,32,256]{2,1,0:T(8,128)S(1)} collective-permute-done((f32[4,32,256]{2,1,0:T(8,128)S(1)}, f32[4,32,256]{2,1,0:T(8,128)S(1)}, u32[]{:S(2)}, u32[]{:S(2)}) %collective-permute-start.8) | collective-permute-done | bytes 131104 | tf_op jit(solution)/shard_map/ppermute | solution.py:20
  307.2 3.9 %collective-permute-start.11 = (f32[40,4,256]{2,1,0:T(4,128)S(1)}, f32[40,4,256]{2,1,0:T(4,128)S(1)}, u32[]{:S(2)}, u32[]{:S(2)}) collective-permute-start(f32[40,4,256]{2,1,0:T(4,128)S(1)} %get-tuple-element.21), channel_id=1, source_target_pairs={{0,1},{1,2},{2,3},{3,4},{4,5},{5,6},{6,7},{8,9},{9,10},{10,11},{11... | collective-permute-start | bytes 491528 | tf_op jit(solution)/shard_map/ppermute | solution.py:17
  312.8 3.7 collective-permute-done.11
  318.5 12.1 %fusion.70 = (f32[32,32,256]{2,1,0:T(8,128)S(1)}, f32[32,32,256]{2,1,0:T(8,128)}, f32[32,32,256]{2,1,0:T(8,128)}) fusion(f32[32,32,256]{2,1,0:T(8,128)S(1)} %copy-done.3, f32[32,32,256]{2,1,0:T(8,128)S(1)} %get-tuple-element.8, f32[]{:T(128)} %bitcast.12, f32[256]{0:T(256)S(1)} %compare_convert_fusion, f32[32,32]{1,0:T(8,128)S(1)} %broadcast_multiply_fusion, ...), kind=kLoop, calls=%fused_computation.133 | loop fusion | flops 17039360 | bytes 48419848 | tf_op jit(solution)/shard_map/add | solution.py:115
  336.5 2.8 collective-permute-start.13
  342.3 3.8 %collective-permute-done.12 = f32[4,32,256]{2,1,0:T(8,128)S(1)} collective-permute-done((f32[4,32,256]{2,1,0:T(8,128)S(1)}, f32[4,32,256]{2,1,0:T(8,128)S(1)}, u32[]{:S(2)}, u32[]{:S(2)}) %collective-permute-start.12) | collective-permute-done | bytes 131104 | tf_op jit(solution)/shard_map/ppermute | solution.py:20
  348.2 4.1 %collective-permute-start.15 = (f32[40,4,256]{2,1,0:T(4,128)S(1)}, f32[40,4,256]{2,1,0:T(4,128)S(1)}, u32[]{:S(2)}, u32[]{:S(2)}) collective-permute-start(f32[40,4,256]{2,1,0:T(4,128)S(1)} %get-tuple-element.17), channel_id=1, source_target_pairs={{0,1},{1,2},{2,3},{3,4},{4,5},{5,6},{6,7},{8,9},{9,10},{10,11},{11... | collective-permute-start | bytes 491528 | tf_op jit(solution)/shard_map/ppermute | solution.py:17
  354.0 3.5 collective-permute-done.15
  359.5 11.0 %add_bitcast_fusion = (f32[1,32,32,256]{3,2,1,0:T(8,128)}, f32[32,32,256]{2,1,0:T(8,128)S(1)}, f32[32,32,256]{2,1,0:T(8,128)}) fusion(f32[32,32,256]{2,1,0:T(8,128)S(1)} %multiply_add_fusion.3, f32[32,32,256]{2,1,0:T(8,128)S(1)} %multiply_add_fusion.1, s32[]{:T(128)S(6)} %min.6, bf16[512,32,256]{2,1,0:T(8,128)(2,1)S(1)} %bitcast.35, ...), kind=kLoop, calls=%fused_computation.204 | loop fusion | flops 15204352 | bytes 40026116 | tf_op jit(solution)/shard_map/broadcast_in_dim | solution.py:117
  370.4 4.0 %fusion.72 = f32[1,32,32,256]{3,2,1,0:T(8,128)} fusion(f32[32,32,256]{2,1,0:T(8,128)} %get-tuple-element.4, f32[32,32,256]{2,1,0:T(8,128)S(1)} %get-tuple-element.3, f32[32,32,256]{2,1,0:T(8,128)S(1)} %get-tuple-element.8, f32[32,32,256]{2,1,0:T(8,128)S(1)} %get-tuple-element.5, f32[]{:T(128)} %bitcast.13, f32[256]{0:T(256)S(1)} %compare_convert_fusion, ...), kind=kLoop, calls=%fused_computation.135 | loop fusion | flops 4718592 | bytes 30413832 | tf_op jit(solution)/shard_map/broadcast_in_dim | solution.py:117
  (78 shorter events, 59.1 us)
Async XLA Ops:
  7.2 9.3 %copy-start = (f32[1,32,32,256]{3,2,1,0:T(8,128)S(1)}, f32[1,32,32,256]{3,2,1,0:T(8,128)}, u32[]{:S(2)}) copy-start(f32[1,32,32,256]{3,2,1,0:T(8,128)} %param.18) | copy-start | bytes 3145732
  7.2 77.9 %all-gather.4.cloned.1.call-start = ((), (), s32[]{:S(2)}) async-start(), calls=%async_computation | async-start | bytes 8912896 | tf_op jit(solution)/shard_map/all_gather | solution.py:93
  7.9 150.5 %all-gather.6.cloned.1.call-start = ((), (), s32[]{:S(2)}) async-start(), calls=%async_computation.1 | async-start | bytes 8912896 | tf_op jit(solution)/shard_map/all_gather | solution.py:94
  8.7 223.1 %all-gather.8.cloned.1.call-start = ((), (), s32[]{:S(2)}) async-start(), calls=%async_computation.2 | async-start | bytes 8912896 | tf_op jit(solution)/shard_map/all_gather | solution.py:95
  9.4 13.9 %collective-permute-start.1 = (f32[4,32,256]{2,1,0:T(8,128)S(1)}, f32[4,32,256]{2,1,0:T(8,128)S(1)}, u32[]{:S(2)}, u32[]{:S(2)}) collective-permute-start(f32[4,32,256]{2,1,0:T(8,128)S(1)} %get-tuple-element.68), channel_id=1, source_target_pairs={{0,8},{8,16},{16,24},{1,9},{9,17},{17,25},{2,10},{10,18},{18,26},{... | collective-permute-start | bytes 393224 | tf_op jit(solution)/shard_map/ppermute | solution.py:17
  13.3 10.1 %collective-permute-start = (f32[4,32,256]{2,1,0:T(8,128)S(1)}, f32[4,32,256]{2,1,0:T(8,128)S(1)}, u32[]{:S(2)}, u32[]{:S(2)}) collective-permute-start(f32[4,32,256]{2,1,0:T(8,128)S(1)} %get-tuple-element.69), channel_id=1, source_target_pairs={{8,0},{16,8},{24,16},{9,1},{17,9},{25,17},{10,2},{18,10},{26,18},{... | collective-permute-start | bytes 393224 | tf_op jit(solution)/shard_map/ppermute | solution.py:20
  23.3 8.7 %copy-start.4 = (f32[1,4]{1,0:T(1,128)S(1)}, f32[1,4]{1,0:T(1,128)}, u32[]{:S(2)}) copy-start(f32[1,4]{1,0:T(1,128)} %param.15) | copy-start | bytes 52
  23.4 9.4 %collective-permute-start.2 = (f32[40,4,256]{2,1,0:T(4,128)S(1)}, f32[40,4,256]{2,1,0:T(4,128)S(1)}, u32[]{:S(2)}, u32[]{:S(2)}) collective-permute-start(f32[40,4,256]{2,1,0:T(4,128)S(1)} %get-tuple-element.28), channel_id=1, source_target_pairs={{1,0},{2,1},{3,2},{4,3},{5,4},{6,5},{7,6},{9,8},{10,9},{11,10},{12... | collective-permute-start | bytes 491528 | tf_op jit(solution)/shard_map/ppermute | solution.py:20
  28.4 9.4 %collective-permute-start.3 = (f32[40,4,256]{2,1,0:T(4,128)S(1)}, f32[40,4,256]{2,1,0:T(4,128)S(1)}, u32[]{:S(2)}, u32[]{:S(2)}) collective-permute-start(f32[40,4,256]{2,1,0:T(4,128)S(1)} %get-tuple-element.29), channel_id=1, source_target_pairs={{0,1},{1,2},{2,3},{3,4},{4,5},{5,6},{6,7},{8,9},{9,10},{10,11},{11... | collective-permute-start | bytes 491528 | tf_op jit(solution)/shard_map/ppermute | solution.py:17
  231.8 12.9 %slice-start = ((s8[8388608]{0:T(1024)(128)(4,1)}), s8[4194304]{0:T(1024)(128)(4,1)S(1)}, s32[]{:S(2)}) async-start(s8[8388608]{0:T(1024)(128)(4,1)} %bitcast.34), calls=%async_computation.3 | async-start | bytes 8388608
  231.8 12.9 %slice-start.1 = ((s8[8388608]{0:T(1024)(128)(4,1)}), s8[4194304]{0:T(1024)(128)(4,1)S(1)}, s32[]{:S(2)}) async-start(s8[8388608]{0:T(1024)(128)(4,1)} %bitcast.34), calls=%async_computation.4 | async-start | bytes 8388608
  244.7 32.4 %copy-start.2 = (f32[32,32,256]{2,1,0:T(8,128)}, f32[32,32,256]{2,1,0:T(8,128)S(1)}, u32[]{:S(2)}) copy-start(f32[32,32,256]{2,1,0:T(8,128)S(1)} %get-tuple-element.11) | copy-start | bytes 3145732
  250.9 5.1 %collective-permute-start.5 = (f32[4,32,256]{2,1,0:T(8,128)S(1)}, f32[4,32,256]{2,1,0:T(8,128)S(1)}, u32[]{:S(2)}, u32[]{:S(2)}) collective-permute-start(f32[4,32,256]{2,1,0:T(8,128)S(1)} %get-tuple-element.58), channel_id=1, source_target_pairs={{0,8},{8,16},{16,24},{1,9},{9,17},{17,25},{2,10},{10,18},{18,26},{... | collective-permute-start | bytes 393224 | tf_op jit(solution)/shard_map/ppermute | solution.py:17
  252.8 7.4 %collective-permute-start.4 = (f32[4,32,256]{2,1,0:T(8,128)S(1)}, f32[4,32,256]{2,1,0:T(8,128)S(1)}, u32[]{:S(2)}, u32[]{:S(2)}) collective-permute-start(f32[4,32,256]{2,1,0:T(8,128)S(1)} %get-tuple-element.59), channel_id=1, source_target_pairs={{8,0},{16,8},{24,16},{9,1},{17,9},{25,17},{10,2},{18,10},{26,18},{... | collective-permute-start | bytes 393224 | tf_op jit(solution)/shard_map/ppermute | solution.py:20
  260.2 9.3 %collective-permute-start.6 = (f32[40,4,256]{2,1,0:T(4,128)S(1)}, f32[40,4,256]{2,1,0:T(4,128)S(1)}, u32[]{:S(2)}, u32[]{:S(2)}) collective-permute-start(f32[40,4,256]{2,1,0:T(4,128)S(1)} %get-tuple-element.24), channel_id=1, source_target_pairs={{1,0},{2,1},{3,2},{4,3},{5,4},{6,5},{7,6},{9,8},{10,9},{11,10},{12... | collective-permute-start | bytes 491528 | tf_op jit(solution)/shard_map/ppermute | solution.py:20
  265.7 9.3 %collective-permute-start.7 = (f32[40,4,256]{2,1,0:T(4,128)S(1)}, f32[40,4,256]{2,1,0:T(4,128)S(1)}, u32[]{:S(2)}, u32[]{:S(2)}) collective-permute-start(f32[40,4,256]{2,1,0:T(4,128)S(1)} %get-tuple-element.25), channel_id=1, source_target_pairs={{0,1},{1,2},{2,3},{3,4},{4,5},{5,6},{6,7},{8,9},{9,10},{10,11},{11... | collective-permute-start | bytes 491528 | tf_op jit(solution)/shard_map/ppermute | solution.py:17
  295.0 6.2 %collective-permute-start.9 = (f32[4,32,256]{2,1,0:T(8,128)S(1)}, f32[4,32,256]{2,1,0:T(8,128)S(1)}, u32[]{:S(2)}, u32[]{:S(2)}) collective-permute-start(f32[4,32,256]{2,1,0:T(8,128)S(1)} %get-tuple-element.48), channel_id=1, source_target_pairs={{0,8},{8,16},{16,24},{1,9},{9,17},{17,25},{2,10},{10,18},{18,26},{... | collective-permute-start | bytes 393224 | tf_op jit(solution)/shard_map/ppermute | solution.py:17
  298.3 6.9 %collective-permute-start.8 = (f32[4,32,256]{2,1,0:T(8,128)S(1)}, f32[4,32,256]{2,1,0:T(8,128)S(1)}, u32[]{:S(2)}, u32[]{:S(2)}) collective-permute-start(f32[4,32,256]{2,1,0:T(8,128)S(1)} %get-tuple-element.49), channel_id=1, source_target_pairs={{8,0},{16,8},{24,16},{9,1},{17,9},{25,17},{10,2},{18,10},{26,18},{... | collective-permute-start | bytes 393224 | tf_op jit(solution)/shard_map/ppermute | solution.py:20
  305.2 7.5 %collective-permute-start.10 = (f32[40,4,256]{2,1,0:T(4,128)S(1)}, f32[40,4,256]{2,1,0:T(4,128)S(1)}, u32[]{:S(2)}, u32[]{:S(2)}) collective-permute-start(f32[40,4,256]{2,1,0:T(4,128)S(1)} %get-tuple-element.20), channel_id=1, source_target_pairs={{1,0},{2,1},{3,2},{4,3},{5,4},{6,5},{7,6},{9,8},{10,9},{11,10},{12... | collective-permute-start | bytes 491528 | tf_op jit(solution)/shard_map/ppermute | solution.py:20
  307.2 9.3 %collective-permute-start.11 = (f32[40,4,256]{2,1,0:T(4,128)S(1)}, f32[40,4,256]{2,1,0:T(4,128)S(1)}, u32[]{:S(2)}, u32[]{:S(2)}) collective-permute-start(f32[40,4,256]{2,1,0:T(4,128)S(1)} %get-tuple-element.21), channel_id=1, source_target_pairs={{0,1},{1,2},{2,3},{3,4},{4,5},{5,6},{6,7},{8,9},{9,10},{10,11},{11... | collective-permute-start | bytes 491528 | tf_op jit(solution)/shard_map/ppermute | solution.py:17
  336.5 5.8 %collective-permute-start.13 = (f32[4,32,256]{2,1,0:T(8,128)S(1)}, f32[4,32,256]{2,1,0:T(8,128)S(1)}, u32[]{:S(2)}, u32[]{:S(2)}) collective-permute-start(f32[4,32,256]{2,1,0:T(8,128)S(1)} %get-tuple-element.38), channel_id=1, source_target_pairs={{0,8},{8,16},{16,24},{1,9},{9,17},{17,25},{2,10},{10,18},{18,26},{... | collective-permute-start | bytes 393224 | tf_op jit(solution)/shard_map/ppermute | solution.py:17
  339.3 6.9 %collective-permute-start.12 = (f32[4,32,256]{2,1,0:T(8,128)S(1)}, f32[4,32,256]{2,1,0:T(8,128)S(1)}, u32[]{:S(2)}, u32[]{:S(2)}) collective-permute-start(f32[4,32,256]{2,1,0:T(8,128)S(1)} %get-tuple-element.39), channel_id=1, source_target_pairs={{8,0},{16,8},{24,16},{9,1},{17,9},{25,17},{10,2},{18,10},{26,18},{... | collective-permute-start | bytes 393224 | tf_op jit(solution)/shard_map/ppermute | solution.py:20
  346.2 7.8 %collective-permute-start.14 = (f32[40,4,256]{2,1,0:T(4,128)S(1)}, f32[40,4,256]{2,1,0:T(4,128)S(1)}, u32[]{:S(2)}, u32[]{:S(2)}) collective-permute-start(f32[40,4,256]{2,1,0:T(4,128)S(1)} %get-tuple-element.16), channel_id=1, source_target_pairs={{1,0},{2,1},{3,2},{4,3},{5,4},{6,5},{7,6},{9,8},{10,9},{11,10},{12... | collective-permute-start | bytes 491528 | tf_op jit(solution)/shard_map/ppermute | solution.py:20
  348.2 9.3 %collective-permute-start.15 = (f32[40,4,256]{2,1,0:T(4,128)S(1)}, f32[40,4,256]{2,1,0:T(4,128)S(1)}, u32[]{:S(2)}, u32[]{:S(2)}) collective-permute-start(f32[40,4,256]{2,1,0:T(4,128)S(1)} %get-tuple-element.17), channel_id=1, source_target_pairs={{0,1},{1,2},{2,3},{3,4},{4,5},{5,6},{6,7},{8,9},{9,10},{10,11},{11... | collective-permute-start | bytes 491528 | tf_op jit(solution)/shard_map/ppermute | solution.py:17
  (4 other events, 22.9 us)
Sparse Core Ops, SparseCore 0:
  10.5 74.5 all-gather.3
  87.6 70.8 all-gather.5
  160.9 70.8 all-gather.7
where the time goes:
time: 382 us; the launch traced here: 381 us
  waiting for transfers between devices  224 us (59%)
  other arithmetic  69.8 us (18%)
  starting transfers between devices  43.3 us (11%)
  local copies, waits for them, and re-layouts  29.1 us (8%)
  between operations  14.7 us (4%)
    all_gather x1, waiting for transfers between devices, on_device(): lax.all_gather(delta, ('shot', 'gx'), axis=0, tiled=True)  73.3 us
    all_gather x1, waiting for transfers between devices, on_device(): lax.all_gather(epsilon, ('shot', 'gx'), axis=0, tiled=True)  73.3 us
    all_gather x1, waiting for transfers between devices, on_device(): lax.all_gather(velocity, ('shot', 'gx'), axis=0, tiled=True)  45.4 us
    add x3, other arithmetic, on_device(): p_next = p_next + wavelet[0, step_index] * inner_source  37.1 us
    slice x16, local copies, waits for them, and re-layouts, shifted_up(): return jnp.concatenate([values[..., reach:], filler], -1)  27.2 us
    ppermute x8, starting transfers between devices, with_halo(): lax.ppermute(lax.slice_in_dim(block, block.shape[dim] - width, None, axis...  23.8 us
    ppermute x8, starting transfers between devices, with_halo(): lax.ppermute(lax.slice_in_dim(block, 0, width, axis=dim), axis, backward)  19.5 us
    ppermute x8, waiting for transfers between devices, with_halo(): lax.ppermute(lax.slice_in_dim(block, block.shape[dim] - width, None, axis...  17.9 us
  transfers between devices with their start and end apart: 19, of which 12 were waited for; matrix products, arithmetic and copies ran while one was open for 6% of the time, Pallas kernels for 0%

commit v1 on v0

v1 whole, which is shorter than its diff:
```python
import jax
import jax.numpy as jnp
from jax import lax
from jax.experimental import pallas as pl
from jax.experimental.pallas import tpu as pltpu
from jax.sharding import PartitionSpec as P

STEPS = 4
WEIGHTS = (-205.0 / 72.0, 8.0 / 5.0, -1.0 / 5.0, 8.0 / 315.0, -1.0 / 560.0)
MESH = pl.DeviceIdType.MESH
N = 32
ROWS = (2, 2, 2, 2)
FIRST = (0, 2, 4, 6)
CHUNKS = len(ROWS)
HOPS = (1, 3, 2)


def kernel(
    velocity, epsilon, delta, anchors, sources, wavelet, p_now, p_prev, q_now, q_prev,
    p_out, q_out,
    slab, gathered0, gathered1, gathered2, gathered3, outgoing, window,
    gain_a, gain_b, gain_c, lap, deep, band_hi, band_lo, spot,
    p_m, p_0, p_1, p_2, p_3, p_4, q_m, q_0, q_1, q_2, q_3, q_4,
    rim_out, rim_in,
    load_sem, spread_send, spread_recv, own_sem, x_send, x_recv, core_send, core_recv,
    deal_send, deal_recv, halo_send, halo_recv, store_sem,
):
    gathered = (gathered0, gathered1, gathered2, gathered3)
    p = (p_0, p_1, p_2, p_3, p_4)
    q = (q_0, q_1, q_2, q_3, q_4)
    shot = lax.axis_index("shot")
    gx = lax.axis_index("gx")
    gy = lax.axis_index("gy")
    far = lax.rem(shot + 2, 4)
    mate = shot + 1 - 2 * lax.rem(shot, 2)
    far_mate = lax.rem(mate + 2, 4)
    has_gx = (gx > 0, gx < 3)
    has_gy = (gy > 0, gy < 7)

    def to(s, z, y):
        return (s, z, y)

    barrier = pltpu.get_barrier_semaphore()
    for hop in HOPS:
        pl.semaphore_signal(barrier, inc=1, device_id=to(shot, lax.rem(gx + hop, 4), gy), device_id_type=MESH)
    pl.semaphore_signal(barrier, inc=1, device_id=to(far, gx, gy), device_id_type=MESH)
    pl.semaphore_signal(barrier, inc=1, device_id=to(mate, gx, gy), device_id_type=MESH)
    for side in range(2):
        @pl.when(has_gy[side])
        def _():
            pl.semaphore_signal(barrier, inc=1, device_id=to(shot, gx, gy + 2 * side - 1), device_id_type=MESH)

    loads = []
    def load(src, dst):
        copy = pltpu.make_async_copy(src, dst, load_sem.at[len(loads)])
        copy.start()
        loads.append(copy)
    for m, model in enumerate((velocity, epsilon, delta)):
        load(model, slab.at[m])
    for half in range(2):
        z = pl.ds(128 * half, 128)
        load(p_now.at[0, :, :, z], p_0.at[pl.ds(4, N), half, pl.ds(8, N), :])
    for src, dst in ((p_prev, p_m), (q_now, q_0), (q_prev, q_m)):
        for half in range(2):
            load(src.at[0, :, :, pl.ds(128 * half, 128)], dst.at[:, half])

    pl.semaphore_wait(barrier, 5 + has_gy[0].astype(jnp.int32) + has_gy[1].astype(jnp.int32))

    for m in range(3):
        loads[m].wait()
    spread = {}
    x_copy = {}
    for c in range(CHUNKS):
        for d, hop in enumerate(HOPS):
            z = lax.rem(gx + hop, 4)
            spread[c, d] = pltpu.make_async_remote_copy(
                src_ref=slab.at[:, pl.ds(8 * z + FIRST[c], ROWS[c])],
                dst_ref=gathered[c].at[shot, gx],
                send_sem=spread_send.at[c, d], recv_sem=spread_recv.at[c, d],
                device_id=to(shot, z, gy), device_id_type=MESH)
            spread[c, d].start()
        own_rows = slab.at[:, pl.ds(8 * gx + FIRST[c], ROWS[c])]
        x_copy[c, 0] = pltpu.make_async_remote_copy(
            src_ref=own_rows, dst_ref=gathered[c].at[shot, gx],
            send_sem=x_send.at[c, 0], recv_sem=x_recv.at[c, 0],
            device_id=to(far, gx, gy), device_id_type=MESH)
        x_copy[c, 0].start()
    own = []
    for c in range(CHUNKS):
        own.append(pltpu.make_async_copy(
            slab.at[:, pl.ds(8 * gx + FIRST[c], ROWS[c])], gathered[c].at[shot, gx], own_sem.at[c]))
        own[c].start()

    def x_halo(t, side):
        return pltpu.make_async_remote_copy(
            src_ref=p[t].at[pl.ds(4 if side == 0 else 32, 4), :, pl.ds(8, N), :],
            dst_ref=p[t].at[pl.ds(36 if side == 0 else 0, 4), :, pl.ds(8, N), :],
            send_sem=halo_send.at[t, side], recv_sem=halo_recv.at[t, side],
            device_id=to(shot, gx + 2 * side - 1, gy), device_id_type=MESH)

    def y_halo(t, side):
        return pltpu.make_async_remote_copy(
            src_ref=rim_out.at[t, side], dst_ref=rim_in.at[t, 1 - side],
            send_sem=halo_send.at[t, 2 + side], recv_sem=halo_recv.at[t, 2 + side],
            device_id=to(shot, gx, gy + 2 * side - 1), device_id_type=MESH)

    def send_x(t):
        for side in range(2):
            @pl.when(has_gx[side])
            def _():
                x_halo(t, side).start()

    def send_y(t):
        for side in range(2):
            @pl.when(has_gy[side])
            def _():
                y_halo(t, side).start()

    def await_halos(t):
        for side in range(2):
            @pl.when(has_gx[side])
            def _():
                x_halo(t, 1 - side).wait_recv()
                x_halo(t, side).wait_send()
        for side in range(2):
            @pl.when(has_gy[side])
            def _():
                y_halo(t, 1 - side).wait_recv()
                y_halo(t, side).wait_send()

            @pl.when(jnp.logical_not(has_gy[side]))
            def _():
                rim_in[t, side] = jnp.zeros((N, 2, 4, 128), jnp.float32)

        @pl.loop(0, N)
        def _(x):
            for half in range(2):
                p[t][x + 4, half, 4:8, :] = rim_in[t, 0, x, half]
                p[t][x + 4, half, 40:44, :] = rim_in[t, 1, x, half]

    for side in range(2):
        @pl.when(jnp.logical_not(has_gx[side]))
        def _():
            for t in range(STEPS):
                @pl.loop(0, 4)
                def _(x):
                    for half in range(2):
                        p[t][x + 36 * side, half, 8:40, :] = jnp.zeros((N, 128), jnp.float32)

    row = lax.broadcasted_iota(jnp.int32, (256, 256), 0)
    col = lax.broadcasted_iota(jnp.int32, (256, 256), 1)
    apart = jnp.abs(row - col)
    band = jnp.zeros((256, 256), jnp.float32)
    for k in range(5):
        band = jnp.where(apart == k, jnp.float32(WEIGHTS[k]), band)
    hi = band.astype(jnp.bfloat16)
    band_hi[...] = hi
    band_lo[...] = (band - hi.astype(jnp.float32)).astype(jnp.bfloat16)
    y_at = lax.broadcasted_iota(jnp.int32, (N, 128), 0) + gy * N
    z_at = lax.broadcasted_iota(jnp.int32, (N, 128), 1)
    for half in range(2):
        here = jnp.logical_and(y_at == sources[0, 1], z_at + 128 * half == sources[0, 2])
        spot[half] = jnp.where(here, jnp.float32(1), jnp.float32(0))

    for i in range(3, 5):
        loads[i].wait()

    @pl.loop(0, N)
    def _(x):
        for half in range(2):
            rim_out[0, 0, x, half] = p_0[x + 4, half, 8:12, :]
            rim_out[0, 1, x, half] = p_0[x + 4, half, 36:40, :]
    send_x(0)
    send_y(0)

    core_copy = {}

    def core(c, which, s):
        core_copy[c, which] = pltpu.make_async_remote_copy(
            src_ref=gathered[c].at[s], dst_ref=gathered[c].at[s],
            send_sem=core_send.at[c, which], recv_sem=core_recv.at[c, which],
            device_id=to(mate, gx, gy), device_id_type=MESH)
        core_copy[c, which].start()

    def forward(c):
        for d, hop in enumerate(HOPS):
            spread[c, d].wait_recv()
            z = lax.rem(gx + 4 - hop, 4)
            x_copy[c, d + 1] = pltpu.make_async_remote_copy(
                src_ref=gathered[c].at[shot, z], dst_ref=gathered[c].at[shot, z],
                send_sem=x_send.at[c, d + 1], recv_sem=x_recv.at[c, d + 1],
                device_id=to(far, gx, gy), device_id_type=MESH)
            x_copy[c, d + 1].start()
        own[c].wait()
        core(c, 0, shot)

    forward(0)
    forward(1)

    def depth_term(t):
        @pl.loop(0, N // 4)
        def _(group):
            x = 4 * group
            values = jnp.concatenate(
                [q[t][pl.ds(x, 4), 0].reshape(4 * N, 128), q[t][pl.ds(x, 4), 1].reshape(4 * N, 128)], axis=-1)
            hi = values.astype(jnp.bfloat16)
            lo = (values - hi.astype(jnp.float32)).astype(jnp.bfloat16)
            total = jnp.dot(hi, band_hi[...], preferred_element_type=jnp.float32)
            total = total + jnp.dot(lo, band_hi[...], preferred_element_type=jnp.float32)
            total = total + jnp.dot(hi, band_lo[...], preferred_element_type=jnp.float32)
            deep[pl.ds(x, 4), 0] = total[:, :128].reshape(4, N, 128)
            deep[pl.ds(x, 4), 1] = total[:, 128:].reshape(4, N, 128)

    def laplace(t, x, half):
        total = (2.0 * WEIGHTS[0]) * p[t][x + 4, half, 8:40, :]
        for k in range(1, 5):
            pair = p[t][x + 4 + k, half, 8:40, :] + p[t][x + 4 - k, half, 8:40, :]
            pair = pair + (p[t][x + 4, half, 8 + k:40 + k, :] + p[t][x + 4, half, 8 - k:40 - k, :])
            total = total + WEIGHTS[k] * pair
        return total

    for i in range(5, len(loads)):
        loads[i].wait()
    depth_term(0)
    await_halos(0)

    @pl.loop(0, N)
    def _(x):
        for half in range(2):
            lap[x, half] = laplace(0, x, half)

    for c in range(2, CHUNKS):
        forward(c)

    anchor = anchors[shot]
    shift = lax.rem(anchor, N)
    base = lax.div(anchor, N)
    deal = {}

    def select(c):
        for d in (0, 1, 3, 2):
            x_copy[c, d].wait_recv()
        core(c, 1, far)
        core_copy[c, 0].wait_recv()
        core_copy[c, 1].wait_recv()
        for d, hop in enumerate(HOPS + (0,)):
            z = lax.rem(gx + hop, 4)
            for kk in range(ROWS[c]):
                k = 8 * gx + FIRST[c] + kk
                at = jnp.minimum(base + z + (k < shift).astype(jnp.int32), 15)
                values = gathered[c][lax.div(at, 4), lax.rem(at, 4), :, kk]
                if hop:
                    outgoing[d, :, FIRST[c] + kk] = values
                else:
                    window[:, gx, FIRST[c] + kk] = values
            if hop:
                deal[c, d] = pltpu.make_async_remote_copy(
                    src_ref=outgoing.at[d, :, pl.ds(FIRST[c], ROWS[c])],
                    dst_ref=window.at[:, gx, pl.ds(FIRST[c], ROWS[c])],
                    send_sem=deal_send.at[c, d], recv_sem=deal_recv.at[c, d],
                    device_id=to(shot, z, gy), device_id_type=MESH)
                deal[c, d].start()

    def gains(c):
        for d in range(3):
            deal[c, d].wait_recv()

        @pl.loop(0, 4)
        def _(block):
            for kk in range(FIRST[c], FIRST[c] + ROWS[c]):
                speed = window[0, block, kk].astype(jnp.float32)
                eps = window[1, block, kk].astype(jnp.float32)
                dlt = window[2, block, kk].astype(jnp.float32)
                square = speed * speed
                cross = square * jnp.sqrt(1.0 + 2.0 * dlt)
                horiz = square * (1.0 + 2.0 * eps)
                for half in range(2):
                    z = slice(128 * half, 128 * half + 128)
                    gain_a[8 * block + kk, half] = horiz[:, z]
                    gain_b[8 * block + kk, half] = cross[:, z]
                    gain_c[8 * block + kk, half] = square[:, z]

    select(0)
    for c in range(1, CHUNKS):
        select(c)
        gains(c - 1)
    gains(CHUNKS - 1)

    def step(t):
        before_p = p_m if t == 0 else p[t - 1]
        before_q = q_m if t == 0 else q[t - 1]
        off = 0 if t == 0 else 4
        y0 = 0 if t == 0 else 8
        last = t == STEPS - 1

        @pl.loop(0, N)
        def _(x):
            k = lax.rem(x + shift, N)
            amount = jnp.where(x + gx * N == sources[0, 0], wavelet[0, t], jnp.float32(0))
            for half in range(2):
                h = lap[x, half] if t == 0 else laplace(t, x, half)
                z = deep[x, half]
                a, b, c = gain_a[k, half], gain_b[k, half], gain_c[k, half]
                new_p = (2.0 * p[t][x + 4, half, 8:40, :] - before_p[x + off, half, y0:y0 + N, :]) + (a * h + b * z)
                new_p = new_p + amount * spot[half]
                new_q = (2.0 * q[t][x, half] - before_q[x, half]) + (b * h + c * z)
                q[t + 1][x, half] = new_q
                if last:
                    p[t + 1][x, half] = new_p
                else:
                    p[t + 1][x + 4, half, 8:40, :] = new_p
                    rim_out[t + 1, 0, x, half] = new_p[0:4]
                    rim_out[t + 1, 1, x, half] = new_p[28:32]

    for t in range(STEPS):
        if t > 0:
            depth_term(t)
            await_halos(t)
        step(t)
        if t < STEPS - 1:
            send_x(t + 1)
            send_y(t + 1)

    stores = []
    for src, dst in ((p_4, p_out), (q_4, q_out)):
        for half in range(2):
            stores.append(pltpu.make_async_copy(
                src.at[:, half], dst.at[0, :, :, pl.ds(128 * half, 128)], store_sem.at[len(stores)]))
            stores[-1].start()
    for c in range(CHUNKS):
        for d in range(3):
            spread[c, d].wait_send()
            deal[c, d].wait_send()
        for d in range(4):
            x_copy[c, d].wait_send()
        core_copy[c, 0].wait_send()
        core_copy[c, 1].wait_send()
    for copy in stores:
        copy.wait()


def on_device(velocity, epsilon, delta, anchors, sources, wavelet, p_now, p_prev, q_now, q_prev):
    out = jax.ShapeDtypeStruct(p_now.shape, jnp.float32)
    hbm = pl.BlockSpec(memory_space=pl.ANY)
    smem = pl.BlockSpec(memory_space=pltpu.SMEM)
    f32 = jnp.float32
    bf16 = jnp.bfloat16
    block = pltpu.VMEM((N, 2, N, 128), f32)
    padded = pltpu.VMEM((N + 8, 2, N + 16, 128), f32)
    dma = pltpu.SemaphoreType.DMA
    return pl.pallas_call(
        kernel,
        out_shape=(out, out),
        in_specs=[hbm, hbm, hbm, smem, smem, smem, hbm, hbm, hbm, hbm],
        out_specs=(hbm, hbm),
        scratch_shapes=[
            pltpu.VMEM((3, N, N, 256), bf16),
            *[pltpu.VMEM((4, 4, 3, rows, N, 256), bf16) for rows in ROWS],
            pltpu.VMEM((3, 3, 8, N, 256), bf16),
            pltpu.VMEM((3, 4, 8, N, 256), bf16),
            block, block, block, block, block,
            pltpu.VMEM((256, 256), bf16), pltpu.VMEM((256, 256), bf16), pltpu.VMEM((2, N, 128), f32),
            block, padded, padded, padded, padded, block,
            block, block, block, block, block, block,
            pltpu.VMEM((STEPS, 2, N, 2, 4, 128), f32), pltpu.VMEM((STEPS, 2, N, 2, 4, 128), f32),
            dma((11,)), dma((CHUNKS, 3)), dma((CHUNKS, 3)), dma((CHUNKS,)), dma((CHUNKS, 4)), dma((CHUNKS, 4)),
            dma((CHUNKS, 2)), dma((CHUNKS, 2)), dma((CHUNKS, 3)), dma((CHUNKS, 3)),
            dma((STEPS, 4)), dma((STEPS, 4)), dma((4,)),
        ],
        compiler_params=pltpu.CompilerParams(
            collective_id=0, has_side_effects=True, vmem_limit_bytes=56 << 20),
        name="migrate",
    )(velocity, epsilon, delta, anchors, sources, wavelet, p_now, p_prev, q_now, q_prev)


def solution(mesh):
    field = P("shot", "gx", "gy", None)
    model = P(("shot", "gx"), "gy", None)
    return jax.shard_map(
        on_device,
        mesh=mesh,
        in_specs=(model, model, model, P(), P("shot", None), P("shot", None), field, field, field, field),
        out_specs=(field, field),
        check_vma=False,
    )
```

time: 382 us -> 83.3 us (0.22)
  waiting for transfers between devices: 224 us -> 0 us
  Pallas kernels: 0 us -> 79.1 us
  other arithmetic: 69.8 us -> 0 us
  starting transfers between devices: 43.3 us -> 0 us
  local copies, waits for them, and re-layouts: 29.1 us -> 3.37 us
  between operations: 14.7 us -> 0.65 us
    all_gather x3 -> x0, waiting for transfers between devices: 192 us -> none  [the longest x1 73.3 us: on_device(): lax.all_gather(delta, ('shot', 'gx'), axis=0, tiled=True)]
    pallas_call x0 -> x1, Pallas kernels: none -> 79.1 us  [on_device(): pl.pallas_call(kernel, out_shape=(out, out), in_specs=[hbm, hbm, hbm, sme...]
    add x6 -> x0, other arithmetic: 44.8 us -> none  [the longest x3 37.1 us: on_device(): p_next = p_next + wavelet[0, step_index] * inner_source]
    ppermute x16 -> x0, starting transfers between devices: 43.2 us -> none  [the longest x8 23.8 us: with_halo(): lax.ppermute(lax.slice_in_dim(block, block.shape[dim] - width, None, axis...]
    ppermute x16 -> x0, waiting for transfers between devices: 29.9 us -> none  [the longest x8 17.9 us: with_halo(): lax.ppermute(lax.slice_in_dim(block, block.shape[dim] - width, None, axis...]
    slice x22 -> x0, local copies, waits for them, and re-layouts: 28.5 us -> none  [the longest x16 27.2 us: shifted_up(): return jnp.concatenate([values[..., reach:], filler], -1)]
    broadcast_in_dim x2 -> x0, other arithmetic: 15 us -> none  [on_device(): return (p_field[None], q_field[None])]
    concatenate x4 -> x0, other arithmetic: 7.93 us -> none  [with_halo(): block = jnp.concatenate([low, block, high], axis=dim)]
  transfers between devices with their start and end apart: 19 -> 0, of which waited for: 12 -> 0; matrix products, arithmetic and copies ran while one was open for 6% -> 0% of each run, Pallas kernels for 0% -> 0%
where the time goes in v1:
time: 83.3 us; the launch traced here: 83.1 us
  Pallas kernels  79.1 us (95%)
  local copies, waits for them, and re-layouts  3.37 us (4%)
    pallas_call x1, Pallas kernels, on_device(): pl.pallas_call(kernel, out_shape=(out, out), in_specs=[hbm, hbm, hbm, sme...  79.1 us
    unnamed x4, local copies, waits for them, and re-layouts  3.37 us

profile of v1, /device:TPU:2, one launch (start us, length us, event | category | flops | bytes accessed | tf_op | source)
XLA Modules:
  0.0 83.1 jit_solution(8099030479536778945)
XLA Ops:
  0.6 79.1 %migrate.1 = (f32[1,32,32,256]{3,2,1,0:T(8,128)}, f32[1,32,32,256]{3,2,1,0:T(8,128)}) custom-call(bf16[32,32,256]{2,1,0:T(8,128)(2,1)} %velocity.1, bf16[32,32,256]{2,1,0:T(8,128)(2,1)} %epsilon.1, bf16[32,32,256]{2,1,0:T(8,128)(2,1)} %delta.1, s32[4]{0:T(128)} %anchors.1, s32[1,3]{1,0:T(1,128)} %sources.1, f32[1,4]{1,0:T(1,128)} %wavelet.1, ...), custom_call_target="tpu_custom_call" | custom-call | tf_op jit(solution)/shard_map/migrate/pallas_call | solution.py:351
  79.8 0.0 copy-start
  79.8 2.4 %copy.14 = f32[1,32,32,256]{3,2,1,0:T(8,128)} copy(f32[1,32,32,256]{3,2,1,0:T(8,128)} %get-tuple-element.4) | data formatting | bytes 2097152
  82.2 0.0 copy-done
  82.2 1.0 %copy.15 = f32[1,32,32,256]{3,2,1,0:T(8,128)} copy(f32[1,32,32,256]{3,2,1,0:T(8,128)S(1)} %copy-done) | data formatting | bytes 2097152
Async XLA Ops:
  79.8 2.4 %copy-start = (f32[1,32,32,256]{3,2,1,0:T(8,128)S(1)}, f32[1,32,32,256]{3,2,1,0:T(8,128)}, u32[]{:S(2)}) copy-start(f32[1,32,32,256]{3,2,1,0:T(8,128)} %get-tuple-element.5) | copy-start | bytes 3145732

commit v2 on v1

--- a/solution.py
+++ b/solution.py
@@ -9,8 +9,8 @@
 WEIGHTS = (-205.0 / 72.0, 8.0 / 5.0, -1.0 / 5.0, 8.0 / 315.0, -1.0 / 560.0)
 MESH = pl.DeviceIdType.MESH
 N = 32
-ROWS = (2, 2, 2, 2)
-FIRST = (0, 2, 4, 6)
+ROWS = (2, 2, 2, 1, 1)
+FIRST = tuple(sum(ROWS[:c]) for c in range(len(ROWS)))
 CHUNKS = len(ROWS)
 HOPS = (1, 3, 2)
 
@@ -18,16 +18,17 @@
 def kernel(
     velocity, epsilon, delta, anchors, sources, wavelet, p_now, p_prev, q_now, q_prev,
     p_out, q_out,
-    slab, gathered0, gathered1, gathered2, gathered3, outgoing, window,
+    slab, *scratch,
+):
+    gathered = scratch[:CHUNKS]
+    (outgoing, window,
     gain_a, gain_b, gain_c, lap, deep, band_hi, band_lo, spot,
-    p_m, p_0, p_1, p_2, p_3, p_4, q_m, q_0, q_1, q_2, q_3, q_4,
-    rim_out, rim_in,
+    p_m, p_0, p_1, p_2, p_3, q_m, q_0, q_1, q_2, q_3,
+    stage, corner, x_out, x_in, y_out, y_in,
     load_sem, spread_send, spread_recv, own_sem, x_send, x_recv, core_send, core_recv,
-    deal_send, deal_recv, halo_send, halo_recv, store_sem,
-):
-    gathered = (gathered0, gathered1, gathered2, gathered3)
-    p = (p_0, p_1, p_2, p_3, p_4)
-    q = (q_0, q_1, q_2, q_3, q_4)
+    deal_send, deal_recv, halo_send, halo_recv) = scratch[CHUNKS:]
+    p = (p_0, p_1, p_2, p_3)
+    q = (q_0, q_1, q_2, q_3)
     shot = lax.axis_index("shot")
     gx = lax.axis_index("gx")
     gy = lax.axis_index("gy")
@@ -70,7 +71,7 @@
         loads[m].wait()
     spread = {}
     x_copy = {}
-    for c in range(CHUNKS):
+    def scatter(c):
         for d, hop in enumerate(HOPS):
             z = lax.rem(gx + hop, 4)
             spread[c, d] = pltpu.make_async_remote_copy(
@@ -79,12 +80,18 @@
                 send_sem=spread_send.at[c, d], recv_sem=spread_recv.at[c, d],
                 device_id=to(shot, z, gy), device_id_type=MESH)
             spread[c, d].start()
+
+    def cross_own(c):
         own_rows = slab.at[:, pl.ds(8 * gx + FIRST[c], ROWS[c])]
         x_copy[c, 0] = pltpu.make_async_remote_copy(
             src_ref=own_rows, dst_ref=gathered[c].at[shot, gx],
             send_sem=x_send.at[c, 0], recv_sem=x_recv.at[c, 0],
             device_id=to(far, gx, gy), device_id_type=MESH)
         x_copy[c, 0].start()
+
+    for c in range(CHUNKS):
+        scatter(c)
+        cross_own(c)
     own = []
     for c in range(CHUNKS):
         own.append(pltpu.make_async_copy(
@@ -93,25 +100,52 @@
 
     def x_halo(t, side):
         return pltpu.make_async_remote_copy(
-            src_ref=p[t].at[pl.ds(4 if side == 0 else 32, 4), :, pl.ds(8, N), :],
-            dst_ref=p[t].at[pl.ds(36 if side == 0 else 0, 4), :, pl.ds(8, N), :],
+            src_ref=x_out.at[t, side], dst_ref=x_in.at[t, 1 - side],
             send_sem=halo_send.at[t, side], recv_sem=halo_recv.at[t, side],
             device_id=to(shot, gx + 2 * side - 1, gy), device_id_type=MESH)
 
     def y_halo(t, side):
         return pltpu.make_async_remote_copy(
-            src_ref=rim_out.at[t, side], dst_ref=rim_in.at[t, 1 - side],
+            src_ref=y_out.at[t, side], dst_ref=y_in.at[t, 1 - side],
             send_sem=halo_send.at[t, 2 + side], recv_sem=halo_recv.at[t, 2 + side],
             device_id=to(shot, gx, gy + 2 * side - 1), device_id_type=MESH)
 
-    def send_x(t):
-        for side in range(2):
+    def pack_layers(out, side, layer, half, values):
+        near = 3 if side else 0
+        hi = values.astype(jnp.bfloat16)
+        out[layer, half] = hi
+        if layer == near:
+            out[4, half] = (values - hi.astype(jnp.float32)).astype(jnp.bfloat16)
+
+    def unpack_layers(source, side, half):
+        near = 0 if side else 3
+        layers = [source[layer, half].astype(jnp.float32) for layer in range(4)]
+        layers[near] = layers[near] + source[4, half].astype(jnp.float32)
+        return layers
+
+    def corrections(layers, side):
+        result = []
+        for i in range(4):
+            reach = range(i + 1) if side else range(i, 4)
+            terms = [WEIGHTS[4 + j - i if side else i + 4 - j] * layers[j] for j in reach]
+            total = terms[0]
+            for term in terms[1:]:
+                total = total + term
+            result.append(total)
+        return result
+
+    def send_rims(t):
+        for side in range(2):
+            for half in range(2):
+                for layer in range(4):
+                    pack_layers(x_out.at[t, side], side, layer, half, p[t][4 + 28 * side + layer, half, 8:40, :])
             @pl.when(has_gx[side])
             def _():
                 x_halo(t, side).start()
-
-    def send_y(t):
-        for side in range(2):
+        for side in range(2):
+            for half in range(2):
+                for layer in range(4):
+                    pack_layers(y_out.at[t, side], side, layer, half, stage[side, half, N * layer:N * layer + N, :])
             @pl.when(has_gy[side])
             def _():
                 y_halo(t, side).start()
@@ -128,24 +162,35 @@
                 y_halo(t, 1 - side).wait_recv()
                 y_halo(t, side).wait_send()
 
-            @pl.when(jnp.logical_not(has_gy[side]))
-            def _():
-                rim_in[t, side] = jnp.zeros((N, 2, 4, 128), jnp.float32)
-
-        @pl.loop(0, N)
-        def _(x):
-            for half in range(2):
-                p[t][x + 4, half, 4:8, :] = rim_in[t, 0, x, half]
-                p[t][x + 4, half, 40:44, :] = rim_in[t, 1, x, half]
+    def y_corrections(t):
+        for side in range(2):
+            for half in range(2):
+                for i, value in enumerate(corrections(unpack_layers(y_in.at[t, side], side, half), side)):
+                    corner[side, half, N * i:N * i + N, :] = value
 
     for side in range(2):
         @pl.when(jnp.logical_not(has_gx[side]))
         def _():
             for t in range(STEPS):
-                @pl.loop(0, 4)
-                def _(x):
-                    for half in range(2):
-                        p[t][x + 36 * side, half, 8:40, :] = jnp.zeros((N, 128), jnp.float32)
+                x_in[t, side] = jnp.zeros((5, 2, N, 128), jnp.bfloat16)
+
+        @pl.when(jnp.logical_not(has_gy[side]))
+        def _():
+            for t in range(STEPS):
+                y_in[t, side] = jnp.zeros((5, 2, N, 128), jnp.bfloat16)
+
+    for t in range(STEPS):
+        @pl.loop(0, 4)
+        def _(x):
+            for half in range(2):
+                p[t][x, half, 8:40, :] = jnp.zeros((N, 128), jnp.float32)
+                p[t][x + 36, half, 8:40, :] = jnp.zeros((N, 128), jnp.float32)
+
+        @pl.loop(0, N)
+        def _(x):
+            for half in range(2):
+                p[t][x + 4, half, 0:8, :] = jnp.zeros((8, 128), jnp.float32)
+                p[t][x + 4, half, 40:48, :] = jnp.zeros((8, 128), jnp.float32)
 
     row = lax.broadcasted_iota(jnp.int32, (256, 256), 0)
     col = lax.broadcasted_iota(jnp.int32, (256, 256), 1)
@@ -168,10 +213,9 @@
     @pl.loop(0, N)
     def _(x):
         for half in range(2):
-            rim_out[0, 0, x, half] = p_0[x + 4, half, 8:12, :]
-            rim_out[0, 1, x, half] = p_0[x + 4, half, 36:40, :]
-    send_x(0)
-    send_y(0)
+            stage[0, half, pl.ds(x, 4, stride=N), :] = p_0[x + 4, half, 8:12, :]
+            stage[1, half, pl.ds(x, 4, stride=N), :] = p_0[x + 4, half, 36:40, :]
+    send_rims(0)
 
     core_copy = {}
 
@@ -194,22 +238,16 @@
         own[c].wait()
         core(c, 0, shot)
 
-    forward(0)
-    forward(1)
 
     def depth_term(t):
-        @pl.loop(0, N // 4)
-        def _(group):
-            x = 4 * group
-            values = jnp.concatenate(
-                [q[t][pl.ds(x, 4), 0].reshape(4 * N, 128), q[t][pl.ds(x, 4), 1].reshape(4 * N, 128)], axis=-1)
-            hi = values.astype(jnp.bfloat16)
-            lo = (values - hi.astype(jnp.float32)).astype(jnp.bfloat16)
-            total = jnp.dot(hi, band_hi[...], preferred_element_type=jnp.float32)
-            total = total + jnp.dot(lo, band_hi[...], preferred_element_type=jnp.float32)
-            total = total + jnp.dot(hi, band_lo[...], preferred_element_type=jnp.float32)
-            deep[pl.ds(x, 4), 0] = total[:, :128].reshape(4, N, 128)
-            deep[pl.ds(x, 4), 1] = total[:, 128:].reshape(4, N, 128)
+        values = jnp.concatenate([q[t][:, 0].reshape(N * N, 128), q[t][:, 1].reshape(N * N, 128)], axis=-1)
+        hi = values.astype(jnp.bfloat16)
+        lo = (values - hi.astype(jnp.float32)).astype(jnp.bfloat16)
+        total = jnp.dot(hi, band_hi[...], preferred_element_type=jnp.float32)
+        total = total + jnp.dot(lo, band_hi[...], preferred_element_type=jnp.float32)
+        total = total + jnp.dot(hi, band_lo[...], preferred_element_type=jnp.float32)
+        deep[:, 0] = total[:, :128].reshape(N, N, 128)
+        deep[:, 1] = total[:, 128:].reshape(N, N, 128)
 
     def laplace(t, x, half):
         total = (2.0 * WEIGHTS[0]) * p[t][x + 4, half, 8:40, :]
@@ -218,19 +256,6 @@
             pair = pair + (p[t][x + 4, half, 8 + k:40 + k, :] + p[t][x + 4, half, 8 - k:40 - k, :])
             total = total + WEIGHTS[k] * pair
         return total
-
-    for i in range(5, len(loads)):
-        loads[i].wait()
-    depth_term(0)
-    await_halos(0)
-
-    @pl.loop(0, N)
-    def _(x):
-        for half in range(2):
-            lap[x, half] = laplace(0, x, half)
-
-    for c in range(2, CHUNKS):
-        forward(c)
 
     anchor = anchors[shot]
     shift = lax.rem(anchor, N)
@@ -280,11 +305,49 @@
                     gain_b[8 * block + kk, half] = cross[:, z]
                     gain_c[8 * block + kk, half] = square[:, z]
 
+    def first_depth():
+        for i in range(5, len(loads)):
+            loads[i].wait()
+        depth_term(0)
+
+    def first_lap():
+        @pl.loop(0, N // 2)
+        def _(pair):
+            for u in range(2):
+                for half in range(2):
+                    lap[2 * pair + u, half] = laplace(0, 2 * pair + u, half)
+
+        await_halos(0)
+        for side in range(2):
+            for half in range(2):
+                for i, value in enumerate(corrections(unpack_layers(x_in.at[0, side], side, half), side)):
+                    lap[28 * side + i, half] = lap[28 * side + i, half] + value
+        y_corrections(0)
+
+        @pl.loop(0, N)
+        def _(x):
+            for half in range(2):
+                for side in range(2):
+                    rows = slice(28 * side, 28 * side + 4)
+                    lap[x, half, rows, :] = lap[x, half, rows, :] + corner[side, half, pl.ds(x, 4, stride=N), :]
+
+    forward(0)
+    forward(1)
+    first_depth()
+    forward(2)
     select(0)
-    for c in range(1, CHUNKS):
-        select(c)
-        gains(c - 1)
-    gains(CHUNKS - 1)
+    forward(3)
+    forward(4)
+    select(1)
+    first_lap()
+    gains(0)
+    select(2)
+    gains(1)
+    select(3)
+    select(4)
+    gains(2)
+    gains(3)
+    gains(4)
 
     def step(t):
         before_p = p_m if t == 0 else p[t - 1]
@@ -293,8 +356,7 @@
         y0 = 0 if t == 0 else 8
         last = t == STEPS - 1
 
-        @pl.loop(0, N)
-        def _(x):
+        def plane(x):
             k = lax.rem(x + shift, N)
             amount = jnp.where(x + gx * N == sources[0, 0], wavelet[0, t], jnp.float32(0))
             for half in range(2):
@@ -304,29 +366,67 @@
                 new_p = (2.0 * p[t][x + 4, half, 8:40, :] - before_p[x + off, half, y0:y0 + N, :]) + (a * h + b * z)
                 new_p = new_p + amount * spot[half]
                 new_q = (2.0 * q[t][x, half] - before_q[x, half]) + (b * h + c * z)
-                q[t + 1][x, half] = new_q
                 if last:
-                    p[t + 1][x, half] = new_p
+                    p_out[0, x, :, 128 * half:128 * half + 128] = new_p
+                    q_out[0, x, :, 128 * half:128 * half + 128] = new_q
                 else:
+                    q[t + 1][x, half] = new_q
                     p[t + 1][x + 4, half, 8:40, :] = new_p
-                    rim_out[t + 1, 0, x, half] = new_p[0:4]
-                    rim_out[t + 1, 1, x, half] = new_p[28:32]
+                    if t == 0:
+                        stage[0, half, pl.ds(x, 4, stride=N), :] = new_p[0:4]
+                        stage[1, half, pl.ds(x, 4, stride=N), :] = new_p[28:32]
+
+        @pl.loop(0, N // 2)
+        def _(pair):
+            plane(2 * pair)
+            plane(2 * pair + 1)
+
+    def add_rims(t):
+        last = t == STEPS - 1
+
+        def bump(x, k, half, first, count, value):
+            rows = slice(first, first + count)
+            add_p = gain_a[k, half, rows, :] * value
+            add_q = gain_b[k, half, rows, :] * value
+            if last:
+                z = slice(128 * half, 128 * half + 128)
+                p_out[0, x, rows, z] = p_out[0, x, rows, z] + add_p
+                q_out[0, x, rows, z] = q_out[0, x, rows, z] + add_q
+                return None
+            lower = slice(8 + first, 8 + first + count)
+            new_p = p[t + 1][x + 4, half, lower, :] + add_p
+            p[t + 1][x + 4, half, lower, :] = new_p
+            q[t + 1][x, half, rows, :] = q[t + 1][x, half, rows, :] + add_q
+            return new_p
+
+        await_halos(t)
+        for side in range(2):
+            for half in range(2):
+                for i, value in enumerate(corrections(unpack_layers(x_in.at[t, side], side, half), side)):
+                    x = 28 * side + i
+                    bump(x, lax.rem(x + shift, N), half, 0, N, value)
+        y_corrections(t)
+
+        @pl.loop(0, N // 2)
+        def _(pair):
+            for u in range(2):
+                x = 2 * pair + u
+                k = lax.rem(x + shift, N)
+                for half in range(2):
+                    for side in range(2):
+                        new_p = bump(x, k, half, 28 * side, 4, corner[side, half, pl.ds(x, 4, stride=N), :])
+                        if not last:
+                            stage[side, half, pl.ds(x, 4, stride=N), :] = new_p
 
     for t in range(STEPS):
         if t > 0:
             depth_term(t)
-            await_halos(t)
         step(t)
+        if t > 0:
+            add_rims(t)
         if t < STEPS - 1:
-            send_x(t + 1)
-            send_y(t + 1)
-
-    stores = []
-    for src, dst in ((p_4, p_out), (q_4, q_out)):
-        for half in range(2):
-            stores.append(pltpu.make_async_copy(
-                src.at[:, half], dst.at[0, :, :, pl.ds(128 * half, 128)], store_sem.at[len(stores)]))
-            stores[-1].start()
+            send_rims(t + 1)
+
     for c in range(CHUNKS):
         for d in range(3):
             spread[c, d].wait_send()
@@ -335,24 +435,24 @@
             x_copy[c, d].wait_send()
         core_copy[c, 0].wait_send()
         core_copy[c, 1].wait_send()
-    for copy in stores:
-        copy.wait()
 
 
 def on_device(velocity, epsilon, delta, anchors, sources, wavelet, p_now, p_prev, q_now, q_prev):
-    out = jax.ShapeDtypeStruct(p_now.shape, jnp.float32)
+    out = pltpu.VMEM(p_now.shape, jnp.float32)
+    vmem = pl.BlockSpec(memory_space=pltpu.VMEM)
     hbm = pl.BlockSpec(memory_space=pl.ANY)
     smem = pl.BlockSpec(memory_space=pltpu.SMEM)
     f32 = jnp.float32
     bf16 = jnp.bfloat16
     block = pltpu.VMEM((N, 2, N, 128), f32)
     padded = pltpu.VMEM((N + 8, 2, N + 16, 128), f32)
+    rims = pltpu.VMEM((STEPS, 2, 5, 2, N, 128), bf16)
     dma = pltpu.SemaphoreType.DMA
     return pl.pallas_call(
         kernel,
         out_shape=(out, out),
         in_specs=[hbm, hbm, hbm, smem, smem, smem, hbm, hbm, hbm, hbm],
-        out_specs=(hbm, hbm),
+        out_specs=(vmem, vmem),
         scratch_shapes=[
             pltpu.VMEM((3, N, N, 256), bf16),
             *[pltpu.VMEM((4, 4, 3, rows, N, 256), bf16) for rows in ROWS],
@@ -360,12 +460,13 @@
             pltpu.VMEM((3, 4, 8, N, 256), bf16),
             block, block, block, block, block,
             pltpu.VMEM((256, 256), bf16), pltpu.VMEM((256, 256), bf16), pltpu.VMEM((2, N, 128), f32),
-            block, padded, padded, padded, padded, block,
-            block, block, block, block, block, block,
-            pltpu.VMEM((STEPS, 2, N, 2, 4, 128), f32), pltpu.VMEM((STEPS, 2, N, 2, 4, 128), f32),
+            block, padded, padded, padded, padded,
+            block, block, block, block, block,
+            pltpu.VMEM((2, 2, 4 * N, 128), f32), pltpu.VMEM((2, 2, 4 * N, 128), f32),
+            rims, rims, rims, rims,
             dma((11,)), dma((CHUNKS, 3)), dma((CHUNKS, 3)), dma((CHUNKS,)), dma((CHUNKS, 4)), dma((CHUNKS, 4)),
             dma((CHUNKS, 2)), dma((CHUNKS, 2)), dma((CHUNKS, 3)), dma((CHUNKS, 3)),
-            dma((STEPS, 4)), dma((STEPS, 4)), dma((4,)),
+            dma((STEPS, 4)), dma((STEPS, 4)),
         ],
         compiler_params=pltpu.CompilerParams(
             collective_id=0, has_side_effects=True, vmem_limit_bytes=56 << 20),

time: 83.3 us -> 71.5 us (0.86)
  Pallas kernels: 79.1 us -> 68.8 us
  local copies, waits for them, and re-layouts: 3.37 us -> 1.94 us
    pallas_call x1, Pallas kernels: 79.1 us -> 68.8 us  [on_device(): pl.pallas_call(kernel, out_shape=(out, out), in_specs=[hbm, hbm, hbm, sme...]
    unnamed x4 -> x2, local copies, waits for them, and re-layouts: 3.37 us -> 1.94 us
where the time goes in v2:
time: 71.5 us; the launch traced here: 71.4 us
  Pallas kernels  68.8 us (96%)
  local copies, waits for them, and re-layouts  1.94 us (3%)
    pallas_call x1, Pallas kernels, on_device(): pl.pallas_call(kernel, out_shape=(out, out), in_specs=[hbm, hbm, hbm, sme...  68.8 us
    unnamed x2, local copies, waits for them, and re-layouts  1.94 us

profile of v2, /device:TPU:2, one launch (start us, length us, event | category | flops | bytes accessed | tf_op | source)
XLA Modules:
  0.0 71.4 jit_solution(17923873106070313216)
XLA Ops:
  0.6 68.8 %migrate.1 = (f32[1,32,32,256]{3,2,1,0:T(8,128)S(1)}, f32[1,32,32,256]{3,2,1,0:T(8,128)S(1)}) custom-call(bf16[32,32,256]{2,1,0:T(8,128)(2,1)} %velocity.1, bf16[32,32,256]{2,1,0:T(8,128)(2,1)} %epsilon.1, bf16[32,32,256]{2,1,0:T(8,128)(2,1)} %delta.1, s32[4]{0:T(128)} %anchors.1, s32[1,3]{1,0:T(1,128)} %sources.1, f32[1,4]{1,0:T(1,128)} %wavelet.1, ...), custom_call_target="tpu_custom_call" | custom-call | tf_op jit(solution)/shard_map/migrate/pallas_call | solution.py:451
  69.5 1.0 %copy.14 = f32[1,32,32,256]{3,2,1,0:T(8,128)} copy(f32[1,32,32,256]{3,2,1,0:T(8,128)S(1)} %get-tuple-element.2) | data formatting | bytes 2097152
  70.5 1.0 %copy.15 = f32[1,32,32,256]{3,2,1,0:T(8,128)} copy(f32[1,32,32,256]{3,2,1,0:T(8,128)S(1)} %get-tuple-element.3) | data formatting | bytes 2097152

commit v3 on v2

v3 whole, which is shorter than its diff:
```python
import jax
import jax.numpy as jnp
from jax import lax
from jax.experimental import pallas as pl
from jax.experimental.pallas import tpu as pltpu
from jax.sharding import PartitionSpec as P

STEPS = 4
WEIGHTS = (-205.0 / 72.0, 8.0 / 5.0, -1.0 / 5.0, 8.0 / 315.0, -1.0 / 560.0)
MESH = pl.DeviceIdType.MESH
N = 32
PIECES = ((0, 0, 32), (1, 0, 32), (2, 0, 32), (3, 0, 16), (3, 16, 16))
CHUNKS = len(PIECES)
HOPS = (1, 3, 2)
PARTNERS = ((0, 1), (1, 1), (0, 3), (1, 3), (0, 2), (1, 2), (1, 0))


def kernel(
    velocity, epsilon, delta, anchors, sources, wavelet, p_now, p_prev, q_now, q_prev,
    p_out, q_out,
    slab, *scratch,
):
    gathered = scratch[:CHUNKS]
    (outgoing, window,
    gain_a, gain_b, gain_c, lap, deep, band_hi, band_lo, spot,
    p_m, p_0, p_1, p_2, p_3, q_m, q_0, q_1, q_2, q_3,
    stage, corner, x_out, x_in, y_out, y_in,
    load_sem, spread_send, spread_recv, own_sem, x_send, x_recv,
    deal_send, deal_recv, halo_send, halo_recv) = scratch[CHUNKS:]
    p = (p_0, p_1, p_2, p_3)
    q = (q_0, q_1, q_2, q_3)
    shot = lax.axis_index("shot")
    gx = lax.axis_index("gx")
    gy = lax.axis_index("gy")
    far = lax.rem(shot + 2, 4)
    mate = shot + 1 - 2 * lax.rem(shot, 2)
    core = lax.rem(shot, 2)
    pair = shot - core
    shots = (shot, mate)
    first_row = (4 * core, 4 - 4 * core)
    has_gx = (gx > 0, gx < 3)
    has_gy = (gy > 0, gy < 7)

    def to(s, z, y):
        return (s, z, y)

    barrier = pltpu.get_barrier_semaphore()
    for hop in HOPS:
        pl.semaphore_signal(barrier, inc=1, device_id=to(shot, lax.rem(gx + hop, 4), gy), device_id_type=MESH)
    pl.semaphore_signal(barrier, inc=1, device_id=to(far, gx, gy), device_id_type=MESH)
    for hop in range(4):
        pl.semaphore_signal(barrier, inc=1, device_id=to(mate, lax.rem(gx + hop, 4), gy), device_id_type=MESH)
    for side in range(2):
        @pl.when(has_gy[side])
        def _():
            pl.semaphore_signal(barrier, inc=1, device_id=to(shot, gx, gy + 2 * side - 1), device_id_type=MESH)

    loads = []
    def load(src, dst):
        copy = pltpu.make_async_copy(src, dst, load_sem.at[len(loads)])
        copy.start()
        loads.append(copy)
    for m, model in enumerate((velocity, epsilon, delta)):
        load(model, slab.at[m])
    for half in range(2):
        z = pl.ds(128 * half, 128)
        load(p_now.at[0, :, :, z], p_0.at[pl.ds(4, N), half, pl.ds(8, N), :])
    for src, dst in ((p_prev, p_m), (q_now, q_0), (q_prev, q_m)):
        for half in range(2):
            load(src.at[0, :, :, pl.ds(128 * half, 128)], dst.at[:, half])

    pl.semaphore_wait(barrier, 8 + has_gy[0].astype(jnp.int32) + has_gy[1].astype(jnp.int32))

    for m in range(3):
        loads[m].wait()
    spread = {}
    x_copy = {}
    def scatter(c):
        for other, hop in PARTNERS:
            z = lax.rem(gx + hop, 4)
            spread[c, other, hop] = pltpu.make_async_remote_copy(
                src_ref=slab.at[:, 8 * z + first_row[other] + PIECES[c][0], pl.ds(PIECES[c][1], PIECES[c][2])],
                dst_ref=gathered[c].at[shot, gx],
                send_sem=spread_send.at[c, other, hop], recv_sem=spread_recv.at[c, other, hop],
                device_id=to(shots[other], z, gy), device_id_type=MESH)
            spread[c, other, hop].start()

    def cross(c, piece, src, dst):
        x_copy[c, piece] = pltpu.make_async_remote_copy(
            src_ref=src, dst_ref=dst, send_sem=x_send.at[c, piece], recv_sem=x_recv.at[c, piece],
            device_id=to(far, gx, gy), device_id_type=MESH)
        x_copy[c, piece].start()

    def own_rows(c):
        return slab.at[:, 8 * gx + first_row[0] + PIECES[c][0], pl.ds(PIECES[c][1], PIECES[c][2])]

    for c in range(CHUNKS):
        scatter(c)
        cross(c, 0, own_rows(c), gathered[c].at[shot, gx])
    own = []
    for c in range(CHUNKS):
        own.append(pltpu.make_async_copy(own_rows(c), gathered[c].at[shot, gx], own_sem.at[c]))
        own[c].start()

    def x_halo(t, side):
        return pltpu.make_async_remote_copy(
            src_ref=x_out.at[t, side], dst_ref=x_in.at[t, 1 - side],
            send_sem=halo_send.at[t, side], recv_sem=halo_recv.at[t, side],
            device_id=to(shot, gx + 2 * side - 1, gy), device_id_type=MESH)

    def y_halo(t, side):
        return pltpu.make_async_remote_copy(
            src_ref=y_out.at[t, side], dst_ref=y_in.at[t, 1 - side],
            send_sem=halo_send.at[t, 2 + side], recv_sem=halo_recv.at[t, 2 + side],
            device_id=to(shot, gx, gy + 2 * side - 1), device_id_type=MESH)

    def pack_layers(out, side, layer, half, values):
        near = 3 if side else 0
        hi = values.astype(jnp.bfloat16)
        out[layer, half] = hi
        if layer == near:
            out[4, half] = (values - hi.astype(jnp.float32)).astype(jnp.bfloat16)

    def unpack_layers(source, side, half):
        near = 0 if side else 3
        layers = [source[layer, half].astype(jnp.float32) for layer in range(4)]
        layers[near] = layers[near] + source[4, half].astype(jnp.float32)
        return layers

    def corrections(layers, side):
        result = []
        for i in range(4):
            reach = range(i + 1) if side else range(i, 4)
            terms = [WEIGHTS[4 + j - i if side else i + 4 - j] * layers[j] for j in reach]
            total = terms[0]
            for term in terms[1:]:
                total = total + term
            result.append(total)
        return result

    def send_y(t):
        for side in range(2):
            for half in range(2):
                for layer in range(4):
                    pack_layers(y_out.at[t, side], side, layer, half, stage[side, half, N * layer:N * layer + N, :])
            @pl.when(has_gy[side])
            def _():
                y_halo(t, side).start()

    def send_x(t):
        for side in range(2):
            for half in range(2):
                for layer in range(4):
                    pack_layers(x_out.at[t, side], side, layer, half, p[t][4 + 28 * side + layer, half, 8:40, :])
            @pl.when(has_gx[side])
            def _():
                x_halo(t, side).start()

    def send_rims(t):
        send_y(t)
        send_x(t)

    def await_x(t):
        for side in range(2):
            @pl.when(has_gx[side])
            def _():
                x_halo(t, 1 - side).wait_recv()

    def await_y(t):
        for side in range(2):
            @pl.when(has_gy[side])
            def _():
                y_halo(t, 1 - side).wait_recv()

    def y_corrections(t):
        for side in range(2):
            for half in range(2):
                for i, value in enumerate(corrections(unpack_layers(y_in.at[t, side], side, half), side)):
                    corner[side, half, N * i:N * i + N, :] = value

    for side in range(2):
        @pl.when(jnp.logical_not(has_gx[side]))
        def _():
            for t in range(STEPS):
                x_in[t, side] = jnp.zeros((5, 2, N, 128), jnp.bfloat16)

        @pl.when(jnp.logical_not(has_gy[side]))
        def _():
            for t in range(STEPS):
                y_in[t, side] = jnp.zeros((5, 2, N, 128), jnp.bfloat16)

    for t in range(STEPS):
        @pl.loop(0, 4)
        def _(x):
            for half in range(2):
                p[t][x, half, 8:40, :] = jnp.zeros((N, 128), jnp.float32)
                p[t][x + 36, half, 8:40, :] = jnp.zeros((N, 128), jnp.float32)

        @pl.loop(0, N)
        def _(x):
            for half in range(2):
                p[t][x + 4, half, 0:8, :] = jnp.zeros((8, 128), jnp.float32)
                p[t][x + 4, half, 40:48, :] = jnp.zeros((8, 128), jnp.float32)

    row = lax.broadcasted_iota(jnp.int32, (256, 256), 0)
    col = lax.broadcasted_iota(jnp.int32, (256, 256), 1)
    apart = jnp.abs(row - col)
    band = jnp.zeros((256, 256), jnp.float32)
    for k in range(5):
        band = jnp.where(apart == k, jnp.float32(WEIGHTS[k]), band)
    hi = band.astype(jnp.bfloat16)
    band_hi[...] = hi
    band_lo[...] = (band - hi.astype(jnp.float32)).astype(jnp.bfloat16)
    y_at = lax.broadcasted_iota(jnp.int32, (N, 128), 0) + gy * N
    z_at = lax.broadcasted_iota(jnp.int32, (N, 128), 1)
    for half in range(2):
        here = jnp.logical_and(y_at == sources[0, 1], z_at + 128 * half == sources[0, 2])
        spot[half] = jnp.where(here, jnp.float32(1), jnp.float32(0))

    for i in range(3, 5):
        loads[i].wait()

    @pl.loop(0, N)
    def _(x):
        for half in range(2):
            stage[0, half, pl.ds(x, 4, stride=N), :] = p_0[x + 4, half, 8:12, :]
            stage[1, half, pl.ds(x, 4, stride=N), :] = p_0[x + 4, half, 36:40, :]
    send_rims(0)

    def forward(c):
        spread[c, 1, 0].wait_recv()
        cross(c, 1, gathered[c].at[mate, gx], gathered[c].at[mate, gx])
        for d, hop in enumerate(HOPS):
            spread[c, 0, hop].wait_recv()
            spread[c, 1, hop].wait_recv()
            z = lax.rem(gx + 4 - hop, 4)
            both = gathered[c].at[pl.ds(pair, 2), z]
            cross(c, d + 2, both, both)
        own[c].wait()

    def depth_term(t):
        values = jnp.concatenate([q[t][:, 0].reshape(N * N, 128), q[t][:, 1].reshape(N * N, 128)], axis=-1)
        hi = values.astype(jnp.bfloat16)
        lo = (values - hi.astype(jnp.float32)).astype(jnp.bfloat16)
        total = jnp.dot(hi, band_hi[...], preferred_element_type=jnp.float32)
        total = total + jnp.dot(lo, band_hi[...], preferred_element_type=jnp.float32)
        total = total + jnp.dot(hi, band_lo[...], preferred_element_type=jnp.float32)
        deep[:, 0] = total[:, :128].reshape(N, N, 128)
        deep[:, 1] = total[:, 128:].reshape(N, N, 128)

    def laplace(t, x, half):
        total = (2.0 * WEIGHTS[0]) * p[t][x + 4, half, 8:40, :]
        for k in range(1, 5):
            pair = p[t][x + 4 + k, half, 8:40, :] + p[t][x + 4 - k, half, 8:40, :]
            pair = pair + (p[t][x + 4, half, 8 + k:40 + k, :] + p[t][x + 4, half, 8 - k:40 - k, :])
            total = total + WEIGHTS[k] * pair
        return total

    bases = [lax.div(anchors[g], N) for g in shots]
    shifts = [lax.rem(anchors[g], N) for g in shots]
    shift = shifts[0]
    deal = {}

    def select(c):
        for piece in range(5):
            x_copy[c, piece].wait_recv()
        for slot, (other, hop) in enumerate(PARTNERS + ((0, 0),)):
            z = lax.rem(gx + hop, 4)
            mine = (other, hop) == (0, 0)
            row = first_row[0] + PIECES[c][0]
            cells = pl.ds(PIECES[c][1], PIECES[c][2])
            at = jnp.minimum(bases[other] + z + (8 * gx + row < shifts[other]).astype(jnp.int32), 15)
            values = gathered[c][lax.div(at, 4), lax.rem(at, 4)]
            if mine:
                window[:, gx, row, cells] = values
            else:
                outgoing[slot, :, PIECES[c][0], cells] = values
                deal[c, slot] = pltpu.make_async_remote_copy(
                    src_ref=outgoing.at[slot, :, PIECES[c][0], cells],
                    dst_ref=window.at[:, gx, row, cells],
                    send_sem=deal_send.at[c, slot], recv_sem=deal_recv.at[c, slot],
                    device_id=to(shots[other], z, gy), device_id_type=MESH)
                deal[c, slot].start()

    def gains(c):
        for slot in range(7):
            deal[c, slot].wait_recv()

        @pl.loop(0, 8)
        def _(block):
            kk, y0, count = PIECES[c]
            cells = slice(y0, y0 + count)
            row = 4 * lax.rem(block, 2) + kk
            speed = window[0, lax.div(block, 2), row, cells].astype(jnp.float32)
            eps = window[1, lax.div(block, 2), row, cells].astype(jnp.float32)
            dlt = window[2, lax.div(block, 2), row, cells].astype(jnp.float32)
            square = speed * speed
            cross_term = square * jnp.sqrt(1.0 + 2.0 * dlt)
            horiz = square * (1.0 + 2.0 * eps)
            for half in range(2):
                z = slice(128 * half, 128 * half + 128)
                gain_a[4 * block + kk, half, cells] = horiz[:, z]
                gain_b[4 * block + kk, half, cells] = cross_term[:, z]
                gain_c[4 * block + kk, half, cells] = square[:, z]

    def first_depth():
        for i in range(5, len(loads)):
            loads[i].wait()
        depth_term(0)

    def first_lap():
        @pl.loop(0, N // 2)
        def _(pair):
            for u in range(2):
                for half in range(2):
                    lap[2 * pair + u, half] = laplace(0, 2 * pair + u, half)

        await_x(0)
        await_y(0)
        for side in range(2):
            for half in range(2):
                for i, value in enumerate(corrections(unpack_layers(x_in.at[0, side], side, half), side)):
                    lap[28 * side + i, half] = lap[28 * side + i, half] + value
        y_corrections(0)

        @pl.loop(0, N)
        def _(x):
            for half in range(2):
                for side in range(2):
                    rows = slice(28 * side, 28 * side + 4)
                    lap[x, half, rows, :] = lap[x, half, rows, :] + corner[side, half, pl.ds(x, 4, stride=N), :]

    forward(0)
    forward(1)
    first_depth()
    forward(2)
    select(0)
    forward(3)
    forward(4)
    select(1)
    first_lap()
    gains(0)
    select(2)
    gains(1)
    select(3)
    select(4)
    gains(2)
    gains(3)
    gains(4)

    def step(t, do_p, do_q):
        before_p = p_m if t == 0 else p[t - 1]
        before_q = q_m if t == 0 else q[t - 1]
        off = 0 if t == 0 else 4
        y0 = 0 if t == 0 else 8
        last = t == STEPS - 1

        def plane(x):
            k = lax.rem(x + shift, N)
            amount = jnp.where(x + gx * N == sources[0, 0], wavelet[0, t], jnp.float32(0))
            for half in range(2):
                h = lap[x, half] if t == 0 else laplace(t, x, half)
                z = deep[x, half]
                b = gain_b[k, half]
                if do_p:
                    new_p = (2.0 * p[t][x + 4, half, 8:40, :] - before_p[x + off, half, y0:y0 + N, :]) + (
                        gain_a[k, half] * h + b * z)
                    new_p = new_p + amount * spot[half]
                    if last:
                        p_out[0, x, :, 128 * half:128 * half + 128] = new_p
                    else:
                        p[t + 1][x + 4, half, 8:40, :] = new_p
                    if t == 0:
                        stage[0, half, pl.ds(x, 4, stride=N), :] = new_p[0:4]
                        stage[1, half, pl.ds(x, 4, stride=N), :] = new_p[28:32]
                if do_q:
                    new_q = (2.0 * q[t][x, half] - before_q[x, half]) + (b * h + gain_c[k, half] * z)
                    if last:
                        q_out[0, x, :, 128 * half:128 * half + 128] = new_q
                    else:
                        q[t + 1][x, half] = new_q

        @pl.loop(0, N // 2)
        def _(pair):
            plane(2 * pair)
            plane(2 * pair + 1)

    def bump_p(t, x, k, half, first, count, value):
        rows = slice(first, first + count)
        add = gain_a[k, half, rows, :] * value
        if t == STEPS - 1:
            z = slice(128 * half, 128 * half + 128)
            p_out[0, x, rows, z] = p_out[0, x, rows, z] + add
        else:
            lower = slice(8 + first, 8 + first + count)
            new_p = p[t + 1][x + 4, half, lower, :] + add
            p[t + 1][x + 4, half, lower, :] = new_p
            if count == 4:
                stage[first // 28, half, pl.ds(x, 4, stride=N), :] = new_p

    def bump_q(t, x, k, half, first, count, value):
        rows = slice(first, first + count)
        add = gain_b[k, half, rows, :] * value
        if t == STEPS - 1:
            z = slice(128 * half, 128 * half + 128)
            q_out[0, x, rows, z] = q_out[0, x, rows, z] + add
        else:
            q[t + 1][x, half, rows, :] = q[t + 1][x, half, rows, :] + add

    def add_x(t, bumps):
        for side in range(2):
            for half in range(2):
                for i, value in enumerate(corrections(unpack_layers(x_in.at[t, side], side, half), side)):
                    x = 28 * side + i
                    for bump in bumps:
                        bump(t, x, lax.rem(x + shift, N), half, 0, N, value)

    def add_y(t, bumps):
        @pl.loop(0, N // 2)
        def _(pair):
            for u in range(2):
                x = 2 * pair + u
                k = lax.rem(x + shift, N)
                for half in range(2):
                    for side in range(2):
                        value = corner[side, half, pl.ds(x, 4, stride=N), :]
                        for bump in bumps:
                            bump(t, x, k, half, 28 * side, 4, value)

    step(0, True, False)
    send_rims(1)
    step(0, False, True)
    for t in range(1, STEPS):
        depth_term(t)
        step(t, True, True)
        await_x(t)
        add_x(t, (bump_p, bump_q))
        await_y(t)
        y_corrections(t)
        if t < STEPS - 1:
            add_y(t, (bump_p,))
            send_rims(t + 1)
            add_y(t, (bump_q,))
        else:
            add_y(t, (bump_p, bump_q))

    for side in range(2):
        @pl.when(has_gx[side])
        def _():
            for t in range(STEPS):
                x_halo(t, side).wait_send()

        @pl.when(has_gy[side])
        def _():
            for t in range(STEPS):
                y_halo(t, side).wait_send()

    for c in range(CHUNKS):
        for slot, (other, hop) in enumerate(PARTNERS):
            spread[c, other, hop].wait_send()
            deal[c, slot].wait_send()
        for piece in range(5):
            x_copy[c, piece].wait_send()


def keep(p_in, q_in, p_out, q_out, sem):
    copies = [pltpu.make_async_copy(p_in, p_out, sem.at[0]), pltpu.make_async_copy(q_in, q_out, sem.at[1])]
    for copy in copies:
        copy.start()
    for copy in copies:
        copy.wait()


def on_device(velocity, epsilon, delta, anchors, sources, wavelet, p_now, p_prev, q_now, q_prev):
    out = pltpu.VMEM(p_now.shape, jnp.float32)
    vmem = pl.BlockSpec(memory_space=pltpu.VMEM)
    hbm = pl.BlockSpec(memory_space=pl.ANY)
    smem = pl.BlockSpec(memory_space=pltpu.SMEM)
    f32 = jnp.float32
    bf16 = jnp.bfloat16
    block = pltpu.VMEM((N, 2, N, 128), f32)
    padded = pltpu.VMEM((N + 8, 2, N + 16, 128), f32)
    rims = pltpu.VMEM((STEPS, 2, 5, 2, N, 128), bf16)
    dma = pltpu.SemaphoreType.DMA
    p_end, q_end = pl.pallas_call(
        kernel,
        out_shape=(out, out),
        in_specs=[hbm, hbm, hbm, smem, smem, smem, hbm, hbm, hbm, hbm],
        out_specs=(vmem, vmem),
        scratch_shapes=[
            pltpu.VMEM((3, N, N, 256), bf16),
            *[pltpu.VMEM((4, 4, 3, count, 256), bf16) for _, _, count in PIECES],
            pltpu.VMEM((7, 3, 4, N, 256), bf16),
            pltpu.VMEM((3, 4, 8, N, 256), bf16),
            block, block, block, block, block,
            pltpu.VMEM((256, 256), bf16), pltpu.VMEM((256, 256), bf16), pltpu.VMEM((2, N, 128), f32),
            block, padded, padded, padded, padded,
            block, block, block, block, block,
            pltpu.VMEM((2, 2, 4 * N, 128), f32), pltpu.VMEM((2, 2, 4 * N, 128), f32),
            rims, rims, rims, rims,
            dma((11,)), dma((CHUNKS, 2, 4)), dma((CHUNKS, 2, 4)), dma((CHUNKS,)), dma((CHUNKS, 5)), dma((CHUNKS, 5)),
            dma((CHUNKS, 7)), dma((CHUNKS, 7)),
            dma((STEPS, 4)), dma((STEPS, 4)),
        ],
        compiler_params=pltpu.CompilerParams(
            collective_id=0, has_side_effects=True, vmem_limit_bytes=56 << 20),
        name="migrate",
    )(velocity, epsilon, delta, anchors, sources, wavelet, p_now, p_prev, q_now, q_prev)
    result = jax.ShapeDtypeStruct(p_now.shape, f32)
    return pl.pallas_call(
        keep,
        out_shape=(result, result),
        in_specs=[vmem, vmem],
        out_specs=(hbm, hbm),
        scratch_shapes=[dma((2,))],
        name="keep",
    )(pltpu.with_memory_space_constraint(p_end, pltpu.VMEM), pltpu.with_memory_space_constraint(q_end, pltpu.VMEM))


def solution(mesh):
    field = P("shot", "gx", "gy", None)
    model = P(("shot", "gx"), "gy", None)
    return jax.shard_map(
        on_device,
        mesh=mesh,
        in_specs=(model, model, model, P(), P("shot", None), P("shot", None), field, field, field, field),
        out_specs=(field, field),
        check_vma=False,
    )
```

time: 71.5 us -> 69.5 us (0.972)
  local copies, waits for them, and re-layouts: 1.94 us -> 0 us
    unnamed x2 -> x0, local copies, waits for them, and re-layouts: 1.94 us -> none
    pallas_call x1, Pallas kernels: 68.8 us -> 67.5 us  [on_device(): pl.pallas_call(kernel, out_shape=(out, out), in_specs=[hbm, hbm, hbm, sme...]
    pallas_call x0 -> x1, Pallas kernels: none -> 1.33 us  [on_device(): pl.pallas_call(keep, out_shape=(result, result), in_specs=[vmem, vmem], o...]
where the time goes in v3:
time: 69.5 us; the launch traced here: 69.4 us
  Pallas kernels  68.8 us (99%)
    pallas_call x1, Pallas kernels, on_device(): pl.pallas_call(kernel, out_shape=(out, out), in_specs=[hbm, hbm, hbm, sme...  67.5 us

profile of v3, /device:TPU:2, one launch (start us, length us, event | category | flops | bytes accessed | tf_op | source)
XLA Modules:
  0.0 69.4 jit_solution(16662522465860425357)
XLA Ops:
  0.6 67.5 %migrate.1 = (f32[1,32,32,256]{3,2,1,0:T(8,128)S(1)}, f32[1,32,32,256]{3,2,1,0:T(8,128)S(1)}) custom-call(bf16[32,32,256]{2,1,0:T(8,128)(2,1)} %velocity.1, bf16[32,32,256]{2,1,0:T(8,128)(2,1)} %epsilon.1, bf16[32,32,256]{2,1,0:T(8,128)(2,1)} %delta.1, s32[4]{0:T(128)} %anchors.1, s32[1,3]{1,0:T(1,128)} %sources.1, f32[1,4]{1,0:T(1,128)} %wavelet.1, ...), custom_call_target="tpu_custom_call" | custom-call | tf_op jit(solution)/shard_map/migrate/pallas_call | solution.py:485
  68.1 1.3 %keep.1 = (f32[1,32,32,256]{3,2,1,0:T(8,128)}, f32[1,32,32,256]{3,2,1,0:T(8,128)}) custom-call(f32[1,32,32,256]{3,2,1,0:T(8,128)S(1)} %get-tuple-element.4.p_in, f32[1,32,32,256]{3,2,1,0:T(8,128)S(1)} %get-tuple-element.5.q_in), custom_call_target="tpu_custom_call" | custom-call | tf_op jit(solution)/shard_map/keep/pallas_call | solution.py:510

commit v4 on v3

--- a/solution.py
+++ b/solution.py
@@ -24,7 +24,7 @@
     (outgoing, window,
     gain_a, gain_b, gain_c, lap, deep, band_hi, band_lo, spot,
     p_m, p_0, p_1, p_2, p_3, q_m, q_0, q_1, q_2, q_3,
-    stage, corner, x_out, x_in, y_out, y_in,
+    stage, corner, face, x_out, x_in, y_out, y_in,
     load_sem, spread_send, spread_recv, own_sem, x_send, x_recv,
     deal_send, deal_recv, halo_send, halo_recv) = scratch[CHUNKS:]
     p = (p_0, p_1, p_2, p_3)
@@ -95,8 +95,9 @@
         return slab.at[:, 8 * gx + first_row[0] + PIECES[c][0], pl.ds(PIECES[c][1], PIECES[c][2])]
 
     for c in range(CHUNKS):
+        cross(c, 0, own_rows(c), gathered[c].at[shot, gx])
+    for c in range(CHUNKS):
         scatter(c)
-        cross(c, 0, own_rows(c), gathered[c].at[shot, gx])
     own = []
     for c in range(CHUNKS):
         own.append(pltpu.make_async_copy(own_rows(c), gathered[c].at[shot, gx], own_sem.at[c]))
@@ -108,23 +109,23 @@
             send_sem=halo_send.at[t, side], recv_sem=halo_recv.at[t, side],
             device_id=to(shot, gx + 2 * side - 1, gy), device_id_type=MESH)
 
-    def y_halo(t, side):
+    def y_halo(t, side, half):
         return pltpu.make_async_remote_copy(
-            src_ref=y_out.at[t, side], dst_ref=y_in.at[t, 1 - side],
-            send_sem=halo_send.at[t, 2 + side], recv_sem=halo_recv.at[t, 2 + side],
+            src_ref=y_out.at[t, side, half], dst_ref=y_in.at[t, 1 - side, half],
+            send_sem=halo_send.at[t, 2 + 2 * side + half], recv_sem=halo_recv.at[t, 2 + 2 * side + half],
             device_id=to(shot, gx, gy + 2 * side - 1), device_id_type=MESH)
 
-    def pack_layers(out, side, layer, half, values):
+    def pack_layers(out, side, layer, values):
         near = 3 if side else 0
         hi = values.astype(jnp.bfloat16)
-        out[layer, half] = hi
+        out[layer] = hi
         if layer == near:
-            out[4, half] = (values - hi.astype(jnp.float32)).astype(jnp.bfloat16)
-
-    def unpack_layers(source, side, half):
+            out[4] = (values - hi.astype(jnp.float32)).astype(jnp.bfloat16)
+
+    def unpack_layers(source, side):
         near = 0 if side else 3
-        layers = [source[layer, half].astype(jnp.float32) for layer in range(4)]
-        layers[near] = layers[near] + source[4, half].astype(jnp.float32)
+        layers = [source[layer].astype(jnp.float32) for layer in range(4)]
+        layers[near] = layers[near] + source[4].astype(jnp.float32)
         return layers
 
     def corrections(layers, side):
@@ -138,26 +139,27 @@
             result.append(total)
         return result
 
-    def send_y(t):
-        for side in range(2):
-            for half in range(2):
-                for layer in range(4):
-                    pack_layers(y_out.at[t, side], side, layer, half, stage[side, half, N * layer:N * layer + N, :])
+    def send_y(t, half):
+        for side in range(2):
+            for layer in range(4):
+                pack_layers(y_out.at[t, side, half], side, layer, stage[side, half, N * layer:N * layer + N, :])
+
             @pl.when(has_gy[side])
             def _():
-                y_halo(t, side).start()
+                y_halo(t, side, half).start()
 
     def send_x(t):
         for side in range(2):
             for half in range(2):
                 for layer in range(4):
-                    pack_layers(x_out.at[t, side], side, layer, half, p[t][4 + 28 * side + layer, half, 8:40, :])
+                    pack_layers(x_out.at[t, side, half], side, layer, p[t][4 + 28 * side + layer, half, 8:40, :])
             @pl.when(has_gx[side])
             def _():
                 x_halo(t, side).start()
 
     def send_rims(t):
-        send_y(t)
+        send_y(t, 0)
+        send_y(t, 1)
         send_x(t)
 
     def await_x(t):
@@ -166,28 +168,25 @@
             def _():
                 x_halo(t, 1 - side).wait_recv()
 
-    def await_y(t):
+    def await_y(t, half):
         for side in range(2):
             @pl.when(has_gy[side])
             def _():
-                y_halo(t, 1 - side).wait_recv()
-
-    def y_corrections(t):
-        for side in range(2):
-            for half in range(2):
-                for i, value in enumerate(corrections(unpack_layers(y_in.at[t, side], side, half), side)):
-                    corner[side, half, N * i:N * i + N, :] = value
+                y_halo(t, 1 - side, half).wait_recv()
+        for side in range(2):
+            for i, value in enumerate(corrections(unpack_layers(y_in.at[t, side, half], side), side)):
+                corner[side, half, N * i:N * i + N, :] = value
 
     for side in range(2):
         @pl.when(jnp.logical_not(has_gx[side]))
         def _():
             for t in range(STEPS):
-                x_in[t, side] = jnp.zeros((5, 2, N, 128), jnp.bfloat16)
+                x_in[t, side] = jnp.zeros((2, 5, N, 128), jnp.bfloat16)
 
         @pl.when(jnp.logical_not(has_gy[side]))
         def _():
             for t in range(STEPS):
-                y_in[t, side] = jnp.zeros((5, 2, N, 128), jnp.bfloat16)
+                y_in[t, side] = jnp.zeros((2, 5, N, 128), jnp.bfloat16)
 
     for t in range(STEPS):
         @pl.loop(0, 4)
@@ -225,7 +224,7 @@
         for half in range(2):
             stage[0, half, pl.ds(x, 4, stride=N), :] = p_0[x + 4, half, 8:12, :]
             stage[1, half, pl.ds(x, 4, stride=N), :] = p_0[x + 4, half, 36:40, :]
-    send_rims(0)
+    send_x(0)
 
     def forward(c):
         spread[c, 1, 0].wait_recv()
@@ -264,6 +263,9 @@
     def select(c):
         for piece in range(5):
             x_copy[c, piece].wait_recv()
+        if c == CHUNKS - 1:
+            send_y(0, 0)
+            send_y(0, 1)
         for slot, (other, hop) in enumerate(PARTNERS + ((0, 0),)):
             z = lax.rem(gx + hop, 4)
             mine = (other, hop) == (0, 0)
@@ -316,12 +318,14 @@
                     lap[2 * pair + u, half] = laplace(0, 2 * pair + u, half)
 
         await_x(0)
-        await_y(0)
-        for side in range(2):
-            for half in range(2):
-                for i, value in enumerate(corrections(unpack_layers(x_in.at[0, side], side, half), side)):
+        for side in range(2):
+            for half in range(2):
+                for i, value in enumerate(corrections(unpack_layers(x_in.at[0, side, half], side), side)):
                     lap[28 * side + i, half] = lap[28 * side + i, half] + value
-        y_corrections(0)
+
+    def first_y():
+        await_y(0, 0)
+        await_y(0, 1)
 
         @pl.loop(0, N)
         def _(x):
@@ -395,8 +399,6 @@
             lower = slice(8 + first, 8 + first + count)
             new_p = p[t + 1][x + 4, half, lower, :] + add
             p[t + 1][x + 4, half, lower, :] = new_p
-            if count == 4:
-                stage[first // 28, half, pl.ds(x, 4, stride=N), :] = new_p
 
     def bump_q(t, x, k, half, first, count, value):
         rows = slice(first, first + count)
@@ -410,39 +412,66 @@
     def add_x(t, bumps):
         for side in range(2):
             for half in range(2):
-                for i, value in enumerate(corrections(unpack_layers(x_in.at[t, side], side, half), side)):
+                for i, value in enumerate(corrections(unpack_layers(x_in.at[t, side, half], side), side)):
                     x = 28 * side + i
                     for bump in bumps:
                         bump(t, x, lax.rem(x + shift, N), half, 0, N, value)
 
-    def add_y(t, bumps):
+    def add_y(t, bumps, halves):
         @pl.loop(0, N // 2)
         def _(pair):
             for u in range(2):
                 x = 2 * pair + u
                 k = lax.rem(x + shift, N)
-                for half in range(2):
+                for half in halves:
                     for side in range(2):
                         value = corner[side, half, pl.ds(x, 4, stride=N), :]
                         for bump in bumps:
                             bump(t, x, k, half, 28 * side, 4, value)
 
+    def each_rim(move, first, last):
+        @pl.loop(first, last)
+        def _(x):
+            for half in range(2):
+                for side in range(2):
+                    move(x, half, side)
+
+    def keep_gain(x, half, side):
+        face[side, half, pl.ds(x, 4, stride=N), :] = gain_a[lax.rem(x + shift, N), half, 28 * side:28 * side + 4, :]
+
+    first_y()
     step(0, True, False)
     send_rims(1)
+    each_rim(keep_gain, 0, N)
     step(0, False, True)
     for t in range(1, STEPS):
         depth_term(t)
         step(t, True, True)
         await_x(t)
         add_x(t, (bump_p, bump_q))
-        await_y(t)
-        y_corrections(t)
-        if t < STEPS - 1:
-            add_y(t, (bump_p,))
-            send_rims(t + 1)
-            add_y(t, (bump_q,))
-        else:
-            add_y(t, (bump_p, bump_q))
+        if t == STEPS - 1:
+            for half in range(2):
+                await_y(t, half)
+                add_y(t, (bump_p, bump_q), (half,))
+            break
+
+        def take(x, half, side):
+            stage[side, half, pl.ds(x, 4, stride=N), :] = p[t + 1][x + 4, half, 8 + 28 * side:12 + 28 * side, :]
+
+        def give(x, half, side):
+            p[t + 1][x + 4, half, 8 + 28 * side:12 + 28 * side, :] = stage[side, half, pl.ds(x, 4, stride=N), :]
+
+        each_rim(take, 0, N)
+        for half in range(2):
+            await_y(t, half)
+            for side in range(2):
+                stage[side, half] = stage[side, half] + face[side, half] * corner[side, half]
+            send_y(t + 1, half)
+        each_rim(give, 0, 4)
+        each_rim(give, 28, 32)
+        send_x(t + 1)
+        each_rim(give, 4, 28)
+        add_y(t, (bump_q,), (0, 1))
 
     for side in range(2):
         @pl.when(has_gx[side])
@@ -453,7 +482,8 @@
         @pl.when(has_gy[side])
         def _():
             for t in range(STEPS):
-                y_halo(t, side).wait_send()
+                y_halo(t, side, 0).wait_send()
+                y_halo(t, side, 1).wait_send()
 
     for c in range(CHUNKS):
         for slot, (other, hop) in enumerate(PARTNERS):
@@ -480,7 +510,7 @@
     bf16 = jnp.bfloat16
     block = pltpu.VMEM((N, 2, N, 128), f32)
     padded = pltpu.VMEM((N + 8, 2, N + 16, 128), f32)
-    rims = pltpu.VMEM((STEPS, 2, 5, 2, N, 128), bf16)
+    rims = pltpu.VMEM((STEPS, 2, 2, 5, N, 128), bf16)
     dma = pltpu.SemaphoreType.DMA
     p_end, q_end = pl.pallas_call(
         kernel,
@@ -496,11 +526,11 @@
             pltpu.VMEM((256, 256), bf16), pltpu.VMEM((256, 256), bf16), pltpu.VMEM((2, N, 128), f32),
             block, padded, padded, padded, padded,
             block, block, block, block, block,
-            pltpu.VMEM((2, 2, 4 * N, 128), f32), pltpu.VMEM((2, 2, 4 * N, 128), f32),
+            pltpu.VMEM((2, 2, 4 * N, 128), f32), pltpu.VMEM((2, 2, 4 * N, 128), f32), pltpu.VMEM((2, 2, 4 * N, 128), f32),
             rims, rims, rims, rims,
             dma((11,)), dma((CHUNKS, 2, 4)), dma((CHUNKS, 2, 4)), dma((CHUNKS,)), dma((CHUNKS, 5)), dma((CHUNKS, 5)),
             dma((CHUNKS, 7)), dma((CHUNKS, 7)),
-            dma((STEPS, 4)), dma((STEPS, 4)),
+            dma((STEPS, 6)), dma((STEPS, 6)),
         ],
         compiler_params=pltpu.CompilerParams(
             collective_id=0, has_side_effects=True, vmem_limit_bytes=56 << 20),

time: 69.5 us -> 66.8 us (0.961)
  Pallas kernels: 68.8 us -> 66.1 us
    pallas_call x1, Pallas kernels: 67.5 us -> 64.7 us  [on_device(): pl.pallas_call(kernel, out_shape=(out, out), in_specs=[hbm, hbm, hbm, sme...]
where the time goes in v4:
time: 66.8 us; the launch traced here: 66.7 us
  Pallas kernels  66.1 us (99%)
    pallas_call x1, Pallas kernels, on_device(): pl.pallas_call(kernel, out_shape=(out, out), in_specs=[hbm, hbm, hbm, sme...  64.7 us

profile of v4, /device:TPU:2, one launch (start us, length us, event | category | flops | bytes accessed | tf_op | source)
XLA Modules:
  0.0 66.7 jit_solution(16480781669625093877)
XLA Ops:
  0.6 64.7 %migrate.1 = (f32[1,32,32,256]{3,2,1,0:T(8,128)S(1)}, f32[1,32,32,256]{3,2,1,0:T(8,128)S(1)}) custom-call(bf16[32,32,256]{2,1,0:T(8,128)(2,1)} %velocity.1, bf16[32,32,256]{2,1,0:T(8,128)(2,1)} %epsilon.1, bf16[32,32,256]{2,1,0:T(8,128)(2,1)} %delta.1, s32[4]{0:T(128)} %anchors.1, s32[1,3]{1,0:T(1,128)} %sources.1, f32[1,4]{1,0:T(1,128)} %wavelet.1, ...), custom_call_target="tpu_custom_call" | custom-call | tf_op jit(solution)/shard_map/migrate/pallas_call | solution.py:515
  65.4 1.3 %keep.1 = (f32[1,32,32,256]{3,2,1,0:T(8,128)}, f32[1,32,32,256]{3,2,1,0:T(8,128)}) custom-call(f32[1,32,32,256]{3,2,1,0:T(8,128)S(1)} %get-tuple-element.4.p_in, f32[1,32,32,256]{3,2,1,0:T(8,128)S(1)} %get-tuple-element.5.q_in), custom_call_target="tpu_custom_call" | custom-call | tf_op jit(solution)/shard_map/keep/pallas_call | solution.py:540

commit v5 on v4

--- a/solution.py
+++ b/solution.py
@@ -9,7 +9,7 @@
 WEIGHTS = (-205.0 / 72.0, 8.0 / 5.0, -1.0 / 5.0, 8.0 / 315.0, -1.0 / 560.0)
 MESH = pl.DeviceIdType.MESH
 N = 32
-PIECES = ((0, 0, 32), (1, 0, 32), (2, 0, 32), (3, 0, 16), (3, 16, 16))
+PIECES = ((0, 0, 32, 0, 3), (1, 0, 32, 0, 3), (2, 0, 32, 0, 3), (3, 0, 16, 0, 3), (3, 16, 16, 0, 2), (3, 16, 16, 2, 1))
 CHUNKS = len(PIECES)
 HOPS = (1, 3, 2)
 PARTNERS = ((0, 1), (1, 1), (0, 3), (1, 3), (0, 2), (1, 2), (1, 0))
@@ -79,7 +79,7 @@
         for other, hop in PARTNERS:
             z = lax.rem(gx + hop, 4)
             spread[c, other, hop] = pltpu.make_async_remote_copy(
-                src_ref=slab.at[:, 8 * z + first_row[other] + PIECES[c][0], pl.ds(PIECES[c][1], PIECES[c][2])],
+                src_ref=slab.at[pl.ds(PIECES[c][3], PIECES[c][4]), 8 * z + first_row[other] + PIECES[c][0], pl.ds(PIECES[c][1], PIECES[c][2])],
                 dst_ref=gathered[c].at[shot, gx],
                 send_sem=spread_send.at[c, other, hop], recv_sem=spread_recv.at[c, other, hop],
                 device_id=to(shots[other], z, gy), device_id_type=MESH)
@@ -92,7 +92,7 @@
         x_copy[c, piece].start()
 
     def own_rows(c):
-        return slab.at[:, 8 * gx + first_row[0] + PIECES[c][0], pl.ds(PIECES[c][1], PIECES[c][2])]
+        return slab.at[pl.ds(PIECES[c][3], PIECES[c][4]), 8 * gx + first_row[0] + PIECES[c][0], pl.ds(PIECES[c][1], PIECES[c][2])]
 
     for c in range(CHUNKS):
         cross(c, 0, own_rows(c), gathered[c].at[shot, gx])
@@ -156,11 +156,6 @@
             @pl.when(has_gx[side])
             def _():
                 x_halo(t, side).start()
-
-    def send_rims(t):
-        send_y(t, 0)
-        send_y(t, 1)
-        send_x(t)
 
     def await_x(t):
         for side in range(2):
@@ -263,7 +258,7 @@
     def select(c):
         for piece in range(5):
             x_copy[c, piece].wait_recv()
-        if c == CHUNKS - 1:
+        if c == CHUNKS - 2:
             send_y(0, 0)
             send_y(0, 1)
         for slot, (other, hop) in enumerate(PARTNERS + ((0, 0),)):
@@ -271,15 +266,16 @@
             mine = (other, hop) == (0, 0)
             row = first_row[0] + PIECES[c][0]
             cells = pl.ds(PIECES[c][1], PIECES[c][2])
+            models = pl.ds(PIECES[c][3], PIECES[c][4])
             at = jnp.minimum(bases[other] + z + (8 * gx + row < shifts[other]).astype(jnp.int32), 15)
             values = gathered[c][lax.div(at, 4), lax.rem(at, 4)]
             if mine:
-                window[:, gx, row, cells] = values
+                window[models, gx, row, cells] = values
             else:
-                outgoing[slot, :, PIECES[c][0], cells] = values
+                outgoing[slot, models, PIECES[c][0], cells] = values
                 deal[c, slot] = pltpu.make_async_remote_copy(
-                    src_ref=outgoing.at[slot, :, PIECES[c][0], cells],
-                    dst_ref=window.at[:, gx, row, cells],
+                    src_ref=outgoing.at[slot, models, PIECES[c][0], cells],
+                    dst_ref=window.at[models, gx, row, cells],
                     send_sem=deal_send.at[c, slot], recv_sem=deal_recv.at[c, slot],
                     device_id=to(shots[other], z, gy), device_id_type=MESH)
                 deal[c, slot].start()
@@ -287,10 +283,12 @@
     def gains(c):
         for slot in range(7):
             deal[c, slot].wait_recv()
+        if PIECES[c][3] + PIECES[c][4] < 3:
+            return
 
         @pl.loop(0, 8)
         def _(block):
-            kk, y0, count = PIECES[c]
+            kk, y0, count = PIECES[c][:3]
             cells = slice(y0, y0 + count)
             row = 4 * lax.rem(block, 2) + kk
             speed = window[0, lax.div(block, 2), row, cells].astype(jnp.float32)
@@ -323,17 +321,6 @@
                 for i, value in enumerate(corrections(unpack_layers(x_in.at[0, side, half], side), side)):
                     lap[28 * side + i, half] = lap[28 * side + i, half] + value
 
-    def first_y():
-        await_y(0, 0)
-        await_y(0, 1)
-
-        @pl.loop(0, N)
-        def _(x):
-            for half in range(2):
-                for side in range(2):
-                    rows = slice(28 * side, 28 * side + 4)
-                    lap[x, half, rows, :] = lap[x, half, rows, :] + corner[side, half, pl.ds(x, 4, stride=N), :]
-
     forward(0)
     forward(1)
     first_depth()
@@ -341,6 +328,7 @@
     select(0)
     forward(3)
     forward(4)
+    forward(5)
     select(1)
     first_lap()
     gains(0)
@@ -348,9 +336,11 @@
     gains(1)
     select(3)
     select(4)
+    select(5)
     gains(2)
     gains(3)
     gains(4)
+    gains(5)
 
     def step(t, do_p, do_q):
         before_p = p_m if t == 0 else p[t - 1]
@@ -439,29 +429,10 @@
     def keep_gain(x, half, side):
         face[side, half, pl.ds(x, 4, stride=N), :] = gain_a[lax.rem(x + shift, N), half, 28 * side:28 * side + 4, :]
 
-    first_y()
-    step(0, True, False)
-    send_rims(1)
-    each_rim(keep_gain, 0, N)
-    step(0, False, True)
-    for t in range(1, STEPS):
-        depth_term(t)
-        step(t, True, True)
-        await_x(t)
-        add_x(t, (bump_p, bump_q))
-        if t == STEPS - 1:
-            for half in range(2):
-                await_y(t, half)
-                add_y(t, (bump_p, bump_q), (half,))
-            break
-
-        def take(x, half, side):
-            stage[side, half, pl.ds(x, 4, stride=N), :] = p[t + 1][x + 4, half, 8 + 28 * side:12 + 28 * side, :]
-
+    def pass_on(t):
         def give(x, half, side):
             p[t + 1][x + 4, half, 8 + 28 * side:12 + 28 * side, :] = stage[side, half, pl.ds(x, 4, stride=N), :]
 
-        each_rim(take, 0, N)
         for half in range(2):
             await_y(t, half)
             for side in range(2):
@@ -471,6 +442,28 @@
         each_rim(give, 28, 32)
         send_x(t + 1)
         each_rim(give, 4, 28)
+
+    step(0, True, False)
+    each_rim(keep_gain, 0, N)
+    pass_on(0)
+    step(0, False, True)
+    add_y(0, (bump_q,), (0, 1))
+    for t in range(1, STEPS):
+        depth_term(t)
+        step(t, True, True)
+        await_x(t)
+        add_x(t, (bump_p, bump_q))
+        if t == STEPS - 1:
+            for half in range(2):
+                await_y(t, half)
+                add_y(t, (bump_p, bump_q), (half,))
+            break
+
+        def take(x, half, side):
+            stage[side, half, pl.ds(x, 4, stride=N), :] = p[t + 1][x + 4, half, 8 + 28 * side:12 + 28 * side, :]
+
+        each_rim(take, 0, N)
+        pass_on(t)
         add_y(t, (bump_q,), (0, 1))
 
     for side in range(2):
@@ -519,7 +512,7 @@
         out_specs=(vmem, vmem),
         scratch_shapes=[
             pltpu.VMEM((3, N, N, 256), bf16),
-            *[pltpu.VMEM((4, 4, 3, count, 256), bf16) for _, _, count in PIECES],
+            *[pltpu.VMEM((4, 4, models, count, 256), bf16) for _, _, count, _, models in PIECES],
             pltpu.VMEM((7, 3, 4, N, 256), bf16),
             pltpu.VMEM((3, 4, 8, N, 256), bf16),
             block, block, block, block, block,

time: 66.8 us -> 66.5 us (level)
  no operation moved by 1% of the time
where the time goes in v5:
time: 66.5 us; the launch traced here: 66.4 us
  Pallas kernels  65.8 us (99%)
    pallas_call x1, Pallas kernels, on_device(): pl.pallas_call(kernel, out_shape=(out, out), in_specs=[hbm, hbm, hbm, sme...  64.4 us
    pallas_call x1, Pallas kernels, on_device(): pl.pallas_call(keep, out_shape=(result, result), in_specs=[vmem, vmem], o...  1.33 us

profile of v5, /device:TPU:2, one launch (start us, length us, event | category | flops | bytes accessed | tf_op | source)
XLA Modules:
  0.0 66.4 jit_solution(12127117843695324775)
XLA Ops:
  0.6 64.4 %migrate.1 = (f32[1,32,32,256]{3,2,1,0:T(8,128)S(1)}, f32[1,32,32,256]{3,2,1,0:T(8,128)S(1)}) custom-call(bf16[32,32,256]{2,1,0:T(8,128)(2,1)} %velocity.1, bf16[32,32,256]{2,1,0:T(8,128)(2,1)} %epsilon.1, bf16[32,32,256]{2,1,0:T(8,128)(2,1)} %delta.1, s32[4]{0:T(128)} %anchors.1, s32[1,3]{1,0:T(1,128)} %sources.1, f32[1,4]{1,0:T(1,128)} %wavelet.1, ...), custom_call_target="tpu_custom_call" | custom-call | tf_op jit(solution)/shard_map/migrate/pallas_call | solution.py:508
  65.1 1.3 %keep.1 = (f32[1,32,32,256]{3,2,1,0:T(8,128)}, f32[1,32,32,256]{3,2,1,0:T(8,128)}) custom-call(f32[1,32,32,256]{3,2,1,0:T(8,128)S(1)} %get-tuple-element.4.p_in, f32[1,32,32,256]{3,2,1,0:T(8,128)S(1)} %get-tuple-element.5.q_in), custom_call_target="tpu_custom_call" | custom-call | tf_op jit(solution)/shard_map/keep/pallas_call | solution.py:533

commit v6 on v5

--- a/solution.py
+++ b/solution.py
@@ -286,8 +286,7 @@
         if PIECES[c][3] + PIECES[c][4] < 3:
             return
 
-        @pl.loop(0, 8)
-        def _(block):
+        def gain_rows(block):
             kk, y0, count = PIECES[c][:3]
             cells = slice(y0, y0 + count)
             row = 4 * lax.rem(block, 2) + kk
@@ -302,6 +301,11 @@
                 gain_a[4 * block + kk, half, cells] = horiz[:, z]
                 gain_b[4 * block + kk, half, cells] = cross_term[:, z]
                 gain_c[4 * block + kk, half, cells] = square[:, z]
+
+        @pl.loop(0, 2)
+        def _(group):
+            for u in range(4):
+                gain_rows(4 * group + u)
 
     def first_depth():
         for i in range(5, len(loads)):
@@ -408,10 +412,10 @@
                         bump(t, x, lax.rem(x + shift, N), half, 0, N, value)
 
     def add_y(t, bumps, halves):
-        @pl.loop(0, N // 2)
+        @pl.loop(0, N // 4)
         def _(pair):
-            for u in range(2):
-                x = 2 * pair + u
+            for u in range(4):
+                x = 4 * pair + u
                 k = lax.rem(x + shift, N)
                 for half in halves:
                     for side in range(2):

time: 66.5 us -> 66.4 us (level)
  no operation moved by 1% of the time
where the time goes in v6:
time: 66.4 us; the launch traced here: 66.3 us
  Pallas kernels  65.7 us (99%)
    pallas_call x1, Pallas kernels, on_device(): pl.pallas_call(kernel, out_shape=(out, out), in_specs=[hbm, hbm, hbm, sme...  64.3 us
    pallas_call x1, Pallas kernels, on_device(): pl.pallas_call(keep, out_shape=(result, result), in_specs=[vmem, vmem], o...  1.33 us

profile of v6, /device:TPU:2, one launch (start us, length us, event | category | flops | bytes accessed | tf_op | source)
XLA Modules:
  0.0 66.3 jit_solution(13944153140209519478)
XLA Ops:
  0.6 64.3 %migrate.1 = (f32[1,32,32,256]{3,2,1,0:T(8,128)S(1)}, f32[1,32,32,256]{3,2,1,0:T(8,128)S(1)}) custom-call(bf16[32,32,256]{2,1,0:T(8,128)(2,1)} %velocity.1, bf16[32,32,256]{2,1,0:T(8,128)(2,1)} %epsilon.1, bf16[32,32,256]{2,1,0:T(8,128)(2,1)} %delta.1, s32[4]{0:T(128)} %anchors.1, s32[1,3]{1,0:T(1,128)} %sources.1, f32[1,4]{1,0:T(1,128)} %wavelet.1, ...), custom_call_target="tpu_custom_call" | custom-call | tf_op jit(solution)/shard_map/migrate/pallas_call | solution.py:512
  65.0 1.3 %keep.1 = (f32[1,32,32,256]{3,2,1,0:T(8,128)}, f32[1,32,32,256]{3,2,1,0:T(8,128)}) custom-call(f32[1,32,32,256]{3,2,1,0:T(8,128)S(1)} %get-tuple-element.4.p_in, f32[1,32,32,256]{3,2,1,0:T(8,128)S(1)} %get-tuple-element.5.q_in), custom_call_target="tpu_custom_call" | custom-call | tf_op jit(solution)/shard_map/keep/pallas_call | solution.py:537
